TPU v7x, 256 devices: a whole 4x4x8 slice. The times are simulated.
256 devices in a mesh: req: 64 (over x, z, core), tp: 4 (over y).
Axes of the slice: x: 4, y: 4, z: 8, core: 2. Of those that a mesh axis runs over, the one named last changes fastest.
Arguments:
- hidden_in: bfloat16 [8192, 2048], P('req', 'tp'), may hold values from -48 to 48
- norm_in_gain: float32 [2048], replicated, may hold values from 0.1 to 1.9
- q_weight: bfloat16 [2048, 2048], P(None, 'tp'), may hold values from -0.125 to 0.125
- k_weight: bfloat16 [2048, 512], P(None, 'tp'), may hold values from -0.125 to 0.125
- v_weight: bfloat16 [2048, 512], P(None, 'tp'), may hold values from -0.125 to 0.125
- q_gain: float32 [128], replicated, may hold values from 0.1 to 1.9
- k_gain: float32 [128], replicated, may hold values from 0.1 to 1.9
- o_weight: bfloat16 [2048, 2048], P('tp'), may hold values from -0.125 to 0.125
- key_pages: bfloat16 [4, 3072, 128, 128], P('tp', 'req'), may hold values from -256 to 256
- value_pages: bfloat16 [4, 3072, 128, 128], P('tp', 'req'), may hold values from -6 to 6
- page_table: int32 [576, 32], P('req'), may hold values from 0 to 47, as said below
- cache_len: int32 [576], P('req'), may hold values from 1 to 4096, as said below
- norm_post_gain: float32 [2048], replicated, may hold values from 0.1 to 1.9
- expert_ids: int32 [8192, 8], P('req'), may hold values from 0 to 127, all different within a row; in each aligned block of 128 rows (0 to 127, 128 to 255, ...) at most 12 rows name the same one
- route_weights: float32 [8192, 8], P('req'), may hold values from 0.02 to 0.25
- gate_weight: bfloat16 [128, 2048, 768], P('req', None, 'tp'), may hold values from -0.125 to 0.125
- up_weight: bfloat16 [128, 2048, 768], P('req', None, 'tp'), may hold values from -0.125 to 0.125
- down_weight: bfloat16 [128, 768, 2048], P('req', 'tp'), may hold values from -0.21875 to 0.21875
Outputs:
- layer_out: bfloat16 [8192, 2048], P('req', 'tp')
Inputs may be any that keep to these rules, and one draw needn't show every extreme that they name: `cache_len`: in each group of 9 consecutive requests one request holds 4096 cached tokens and another exactly 256; the others hold at most 256. `page_table`: for request r of group g = r // 9, entry j with j * 128 below cache_len[r] names the page, among group g's 48 pages of the caches, that holds the request's cached tokens j * 128 to j * 128 + 127; these pages are distinct within a group. Other entries name arbitrary pages of the group and are not read; pages that no read entry names hold unused data. `expert_ids`: among the 128 rows of one group no expert is named more than 12 times.
All inputs are finite; a program needn't handle non-finite values.
Results may differ from a plain program's by a relative error of at most 0.006.
Values may be sent and summed in bfloat16 or wider, within the bound.
A program may use at most 128 MiB of HBM per device.

v0:
```python
import math

import jax
import jax.numpy as jnp
from jax import lax
from jax.sharding import PartitionSpec as P

PAGE = 128
MAXPG = 32
PRE = 120
TOK_DEV = 128
REQS_DEV = 9
POOL = 48


NORM_EPS = 1e-06
ROPE_BASE = 1000000.0


def rms_scale(values, gain_vec):
    mean_square = jnp.mean(values * values, axis=-1, keepdims=True)
    return values * lax.rsqrt(mean_square + NORM_EPS) * gain_vec


def rotate(values, positions):
    half_dim = values.shape[-1] // 2
    exponent = jnp.arange(half_dim, dtype=jnp.float32) * (2.0 / values.shape[-1])
    frequency = jnp.power(jnp.float32(ROPE_BASE), -exponent)
    angles = positions.astype(jnp.float32)[:, None] * frequency[None, :]
    cosine = jnp.cos(angles)[:, None, :]
    sine_val = jnp.sin(angles)[:, None, :]
    front_half = values[..., :half_dim]
    back_half = values[..., half_dim:]
    return jnp.concatenate(
        [front_half * cosine - back_half * sine_val, back_half * cosine + front_half * sine_val],
        axis=-1,
    )


def token_layout(lengths):
    local_idx = jnp.arange(TOK_DEV, dtype=jnp.int32)
    requests = jnp.where(local_idx < PRE, 0, local_idx - PRE + 1)
    offsets = jnp.where(local_idx < PRE, local_idx, 0)
    request_hot = (requests[:, None] == jnp.arange(REQS_DEV, dtype=jnp.int32)[None, :]).astype(
        jnp.int32
    )
    positions = jnp.sum(request_hot * lengths[None, :], axis=1) + offsets
    return (requests, positions)


def page_slots(table, lengths):
    pages_used = (lengths + PAGE - 1) // PAGE
    entry_live = jnp.arange(MAXPG, dtype=jnp.int32)[None, :] < pages_used[:, None]
    page_match = (
        (table[:, :, None] == jnp.arange(POOL, dtype=jnp.int32)[None, None, :])
        & entry_live[:, :, None]
    ).astype(jnp.int32)
    page_owner = jnp.sum(
        page_match * jnp.arange(REQS_DEV, dtype=jnp.int32)[:, None, None], axis=(0, 1)
    )
    page_start = jnp.sum(
        page_match * (jnp.arange(MAXPG, dtype=jnp.int32) * PAGE)[None, :, None], axis=(0, 1)
    )
    page_used = jnp.sum(page_match, axis=(0, 1)) > 0
    owner_length = jnp.sum(page_match * lengths[:, None, None], axis=(0, 1))
    slot_pos = page_start[:, None] + jnp.arange(PAGE, dtype=jnp.int32)[None, :]
    slot_live = page_used[:, None] & (slot_pos < owner_length[:, None])
    slot_owner = jnp.where(slot_live, page_owner[:, None], -1)
    return slot_owner.reshape(POOL * PAGE)


def attend(
    queries, keys_new, values_new, keys_cache, values_cache, requests, positions, slot_owner
):
    inv_root = 1.0 / math.sqrt(queries.shape[-1])
    cache_mask = slot_owner[None, :] == requests[:, None]
    new_mask = (requests[None, :] == requests[:, None]) & (positions[None, :] <= positions[:, None])
    score_cache = (
        jnp.einsum("tkgh,knh->kgtn", queries, keys_cache, preferred_element_type=jnp.float32)
        * inv_root
    )
    score_new = (
        jnp.einsum("tkgh,skh->kgts", queries, keys_new, preferred_element_type=jnp.float32)
        * inv_root
    )
    score_cache = jnp.where(cache_mask[None, None], score_cache, -1e30)
    score_new = jnp.where(new_mask[None, None], score_new, -1e30)
    row_max = jnp.maximum(
        jnp.max(score_cache, axis=-1, keepdims=True), jnp.max(score_new, axis=-1, keepdims=True)
    )
    exp_cache = jnp.where(cache_mask[None, None], jnp.exp(score_cache - row_max), 0.0)
    exp_new = jnp.where(new_mask[None, None], jnp.exp(score_new - row_max), 0.0)
    total = jnp.sum(exp_cache, axis=-1, keepdims=True) + jnp.sum(exp_new, axis=-1, keepdims=True)
    prob_cache = (exp_cache / total).astype(jnp.bfloat16)
    prob_new = (exp_new / total).astype(jnp.bfloat16)
    mixed = jnp.einsum(
        "kgtn,knh->tkgh", prob_cache, values_cache, preferred_element_type=jnp.float32
    )
    mixed = mixed + jnp.einsum(
        "kgts,skh->tkgh", prob_new, values_new, preferred_element_type=jnp.float32
    )
    return mixed.astype(jnp.bfloat16).reshape(queries.shape[0], -1)


def expert_apply(blocks, gate_weight, up_weight, down_weight):
    local_experts = gate_weight.shape[0]
    sources = blocks.shape[0] // local_experts
    slot_count = blocks.shape[1]
    grouped = blocks.reshape(sources, local_experts, slot_count, blocks.shape[2])
    gate_acts = jnp.einsum(
        "sekd,edf->sekf", grouped, gate_weight, preferred_element_type=jnp.float32
    )
    up_acts = jnp.einsum("sekd,edf->sekf", grouped, up_weight, preferred_element_type=jnp.float32)
    hidden_act = (jax.nn.silu(gate_acts) * up_acts).astype(jnp.bfloat16)
    part_sums = jnp.einsum(
        "sekf,efd->sekd", hidden_act, down_weight, preferred_element_type=jnp.float32
    ).astype(jnp.bfloat16)
    return part_sums.reshape(sources * local_experts, slot_count, part_sums.shape[3])


def build_buffer(normed, slot_index, top_count, expert_count, capacity):
    picked = jnp.repeat(normed, top_count, axis=0)
    buffer_rows = (
        jnp.zeros((expert_count * capacity, normed.shape[1]), normed.dtype)
        .at[slot_index]
        .set(picked)
    )
    return buffer_rows.reshape(expert_count, capacity, normed.shape[1])


def weigh_back(returned, slot_index, route_weights, token_count, top_count):
    row_width = returned.shape[2]
    back_rows = returned.reshape(returned.shape[0] * returned.shape[1], row_width)[slot_index]
    weighted = (
        back_rows.astype(jnp.float32) * route_weights.reshape(token_count * top_count)[:, None]
    )
    return jnp.sum(weighted.reshape(token_count, top_count, row_width), axis=1)


def body(
    hidden_in,
    norm_in_gain,
    q_weight,
    k_weight,
    v_weight,
    q_gain,
    k_gain,
    o_weight,
    key_pages,
    value_pages,
    page_table,
    cache_len,
    norm_post_gain,
    expert_ids,
    route_weights,
    gate_weight,
    up_weight,
    down_weight,
):
    req_count = lax.axis_size("req")
    tp_index = lax.axis_index("tp")
    share_width = hidden_in.shape[1]
    head_dim = q_gain.shape[0]
    kv_local = key_pages.shape[0]
    group_size = q_weight.shape[1] // head_dim // kv_local
    token_count = hidden_in.shape[0]
    x_full = lax.all_gather(hidden_in, "tp", axis=1, tiled=True)
    x_float = x_full.astype(jnp.float32)
    normed_in = rms_scale(x_float, norm_in_gain).astype(jnp.bfloat16)
    query_lin = jnp.dot(normed_in, q_weight, preferred_element_type=jnp.float32).reshape(
        token_count, kv_local * group_size, head_dim
    )
    key_lin = jnp.dot(normed_in, k_weight, preferred_element_type=jnp.float32).reshape(
        token_count, kv_local, head_dim
    )
    values_new = (
        jnp.dot(normed_in, v_weight, preferred_element_type=jnp.float32)
        .astype(jnp.bfloat16)
        .reshape(token_count, kv_local, head_dim)
    )
    requests, positions = token_layout(cache_len)
    queries = (
        rotate(rms_scale(query_lin, q_gain), positions)
        .astype(jnp.bfloat16)
        .reshape(token_count, kv_local, group_size, head_dim)
    )
    keys_new = rotate(rms_scale(key_lin, k_gain), positions).astype(jnp.bfloat16)
    slot_owner = page_slots(page_table, cache_len)
    cache_slots = key_pages.shape[1] * key_pages.shape[2]
    keys_cache = key_pages.reshape(kv_local, cache_slots, head_dim)
    values_cache = value_pages.reshape(kv_local, cache_slots, head_dim)
    attended = attend(
        queries, keys_new, values_new, keys_cache, values_cache, requests, positions, slot_owner
    )
    head_part = jnp.dot(attended, o_weight, preferred_element_type=jnp.float32)
    top_count = expert_ids.shape[1]
    expert_count = gate_weight.shape[0] * req_count
    capacity = max(2, 3 * token_count * top_count // (2 * expert_count))
    flat_expert = expert_ids.reshape(token_count * top_count)
    one_hot = (flat_expert[:, None] == jnp.arange(expert_count, dtype=jnp.int32)[None, :]).astype(
        jnp.int32
    )
    slot_rank = jnp.sum((jnp.cumsum(one_hot, axis=0) - one_hot) * one_hot, axis=1)
    slot_index = flat_expert * capacity + slot_rank
    head_sum = lax.psum(head_part.astype(jnp.bfloat16), "tp").astype(jnp.float32)
    residual_full = x_float + head_sum
    normed_post = rms_scale(residual_full, norm_post_gain).astype(jnp.bfloat16)
    residual = lax.dynamic_slice_in_dim(residual_full, tp_index * share_width, share_width, 1)
    send_buffer = build_buffer(normed_post, slot_index, top_count, expert_count, capacity)
    part_sums = expert_apply(
        lax.all_to_all(send_buffer, "req", split_axis=0, concat_axis=0, tiled=True),
        gate_weight,
        up_weight,
        down_weight,
    )
    returned = lax.all_to_all(part_sums, "req", split_axis=0, concat_axis=0, tiled=True)
    moe_term = weigh_back(returned, slot_index, route_weights, token_count, top_count)
    moe_share = lax.psum_scatter(
        moe_term.astype(jnp.bfloat16), "tp", scatter_dimension=1, tiled=True
    ).astype(jnp.float32)
    return (residual + moe_share).astype(jnp.bfloat16)


def solution(mesh):
    return jax.shard_map(
        body,
        mesh=mesh,
        in_specs=(
            P("req", "tp"),
            P(),
            P(None, "tp"),
            P(None, "tp"),
            P(None, "tp"),
            P(),
            P(),
            P("tp", None),
            P("tp", "req", None, None),
            P("tp", "req", None, None),
            P("req", None),
            P("req"),
            P(),
            P("req", None),
            P("req", None),
            P("req", None, "tp"),
            P("req", None, "tp"),
            P("req", "tp", None),
        ),
        out_specs=P("req", "tp"),
        check_vma=False,
    )
```

profile of v0, /device:TPU:1, one launch (start us, length us, event | category | flops | bytes accessed | tf_op | source)
XLA Modules:
  0.0 603.8 jit_solution(2697087782315061524)
XLA Ops:
  6.6 12.9 %all_gather.3 = bf16[128,2048]{1,0:T(8,128)(2,1)S(1)} all-gather(bf16[128,512]{1,0:T(8,128)(2,1)} %param.18), channel_id=1, replica_groups=mesh['req'=64,'tp'=4] {'tp'}, dimensions={1}, use_global_device_ids=true | all-gather | bytes 655360 | tf_op jit(solution)/shard_map/all_gather | solution.py:167
  19.8 2.1 fusion.78
  23.7 1.5 multiply_reduce_fusion.2
  27.1 4.3 fusion
  31.8 3.7 fusion.1
  35.6 4.0 fusion.29
  39.6 1.6 fusion.32
  41.2 1.3 convolution_convert_fusion
  43.9 49.2 %all-reduce.2.cloned.1.call-done = bf16[128,2048]{1,0:T(8,128)(2,1)} async-done(((bf16[128,2048]{1,0:T(8,128)(2,1)}), bf16[128,2048]{1,0:T(8,128)(2,1)}) %all-reduce.2.cloned.1.call-update) | async-done | bytes 524304 | tf_op jit(solution)/shard_map/psum | solution.py:205
  93.1 2.2 convert_add_fusion
  96.6 10.8 %scatter_custom_fusion = bf16[1536,2048]{1,0:T(8,128)(2,1)} fusion(s32[1024]{0:T(1024)S(1)} %bitcast.145, bf16[]{:T(256)} %constant.80.clone.1, bf16[128,2048]{1,0:T(8,128)(2,1)S(1)} %multiply_convert_fusion), kind=kCustom, calls=%fused_computation.16 | custom fusion | bytes 6815746 | tf_op jit(solution)/shard_map/scatter | solution.py:126
  107.4 10.6 %reshape.516 = bf16[128,12,2048]{2,1,0:T(8,128)(2,1)} reshape(bf16[1536,2048]{1,0:T(8,128)(2,1)} %scatter_custom_fusion) | data formatting | bytes 12582912 | tf_op jit(solution)/shard_map/reshape | solution.py:128
  118.1 199.0 %all_to_all.10 = bf16[128,12,2048]{2,1,0:T(8,128)(2,1)S(1)} all-to-all(bf16[128,12,2048]{2,1,0:T(8,128)(2,1)} %reshape.516), channel_id=1, replica_groups=mesh['req'=64,'tp'=4] {'req'}, dimensions={0} | all-to-all | bytes 12582912 | tf_op jit(solution)/shard_map/all_to_all | solution.py:211
  317.1 3.3 copy-done.2
  320.4 8.0 %fusion.7 = f32[2,64,12,192]{3,1,2,0:T(8,128)} fusion(bf16[64,2,12,2048]{3,2,1,0:T(8,128)(2,1)S(1)} %bitcast.140, bf16[2,2048,192]{1,2,0:T(8,128)(2,1)S(1)} %copy-done.12), kind=kOutput, calls=%fused_computation.14 | convolution fusion | flops 1207959552 | bytes 9043968 | tf_op jit(solution)/shard_map/sekd,edf->sekf/dot_general | solution.py:110
  328.4 16.3 %convert_bitcast_fusion = bf16[64,2,12,2048]{3,0,2,1:T(8,128)(2,1)} fusion(bf16[2,192,2048]{2,1,0:T(8,128)(2,1)} %param.35, f32[2,64,12,192]{3,1,2,0:T(8,128)} %fusion.7, bf16[2,2048,192]{1,2,0:T(8,128)(2,1)} %param.34, bf16[64,2,12,2048]{3,2,1,0:T(8,128)(2,1)} %bitcast.141), kind=kOutput, calls=%fused_computation.11 | convolution fusion | flops 2420834304 | bytes 16908288 | tf_op jit(solution)/shard_map/sekf,efd->sekd/dot_general | solution.py:115
  344.7 9.7 %copy.102 = bf16[64,2,12,2048]{3,2,1,0:T(8,128)(2,1)} copy(bf16[64,2,12,2048]{3,0,2,1:T(8,128)(2,1)} %convert_bitcast_fusion) | data formatting | bytes 12582912 | tf_op jit(solution)/shard_map/reshape | solution.py:118
  354.4 6.2 %all-to-all-start.1 = ((bf16[128,12,2048]{2,1,0:T(8,128)(2,1)}), bf16[128,12,2048]{2,1,0:T(8,128)(2,1)}, u32[]{:S(2)}, u32[]{:S(2)}) async-start(bf16[128,12,2048]{2,1,0:T(8,128)(2,1)} %bitcast.139), calls=%async_computation.1 | async-start | bytes 16777216 | tf_op jit(solution)/shard_map/all_to_all | solution.py:216
  360.7 185.6 %all-to-all-done.1 = bf16[128,12,2048]{2,1,0:T(8,128)(2,1)} async-done(((bf16[128,12,2048]{2,1,0:T(8,128)(2,1)}), bf16[128,12,2048]{2,1,0:T(8,128)(2,1)}, u32[]{:S(2)}, u32[]{:S(2)}) %all-to-all-start.1) | async-done | bytes 6291488 | tf_op jit(solution)/shard_map/all_to_all | solution.py:216
  546.3 10.9 %reshape.519 = bf16[1536,2048]{1,0:T(8,128)(2,1)} reshape(bf16[128,12,2048]{2,1,0:T(8,128)(2,1)} %all-to-all-done.1) | data formatting | bytes 12582912 | tf_op jit(solution)/shard_map/reshape | solution.py:133
  557.3 12.6 %gather_fusion = bf16[1024,2048]{1,0:T(8,128)(2,1)} fusion(bf16[1536,2048]{1,0:T(8,128)(2,1)} %reshape.519, s32[1024]{0:T(1024)S(1)} %broadcast_clamp_fusion), kind=kCustom, calls=%fused_computation | custom fusion | bytes 8392704 | tf_op jit(solution)/shard_map/gather | solution.py:133
  569.8 7.3 %fusion.2 = bf16[128,2048]{1,0:T(8,128)(2,1)} fusion(bf16[1024,2048]{1,0:T(8,128)(2,1)} %gather_fusion, f32[128,8]{1,0:T(8,128)S(1)} %copy.88), kind=kLoop, calls=%fused_computation.8 | loop fusion | flops 6029312 | bytes 4722688 | tf_op jit(solution)/shard_map/reduce_sum | solution.py:137
  577.2 17.8 %reduce-scatter.2.cloned.1.call-done = bf16[128,512]{1,0:T(8,128)(2,1)} async-done(((bf16[128,2048]{1,0:T(8,128)(2,1)}), bf16[128,512]{1,0:T(8,128)(2,1)}) %reduce-scatter.2.cloned.1.call-update) | async-done | bytes 131088 | tf_op jit(solution)/shard_map/reduce_scatter | solution.py:218
  595.0 1.7 add_convert_fusion
  (76 shorter events, 7.1 us)
Async XLA Ops:
  6.5 34.7 %copy-start = (bf16[512,2048]{1,0:T(8,128)(2,1)S(1)}, bf16[512,2048]{1,0:T(8,128)(2,1)}, u32[]{:S(2)}) copy-start(bf16[512,2048]{1,0:T(8,128)(2,1)} %param.25) | copy-start | bytes 6291460
  6.5 19.5 %copy-start.10 = (s32[9]{0:T(128)S(1)}, s32[9]{0:T(128)}, u32[]{:S(2)}) copy-start(s32[9]{0:T(128)} %param.29) | copy-start | bytes 112
  6.5 19.0 %copy-start.8 = (f32[128]{0:T(128)S(1)}, f32[128]{0:T(128)}, u32[]{:S(2)}) copy-start(f32[128]{0:T(128)} %param.24) | copy-start | bytes 1540
  6.5 19.5 %copy-start.6 = (s32[9,32]{1,0:T(8,128)S(1)}, s32[9,32]{1,0:T(8,128)}, u32[]{:S(2)}) copy-start(s32[9,32]{1,0:T(8,128)} %param.28) | copy-start | bytes 3460
  6.5 20.3 %copy-start.9 = (f32[128]{0:T(128)S(1)}, f32[128]{0:T(128)}, u32[]{:S(2)}) copy-start(f32[128]{0:T(128)} %param.23) | copy-start | bytes 1540
  6.5 86.6 %all-reduce.2.cloned.1.call-start = ((), (), s32[]{:S(2)}) async-start(), calls=%async_computation.3 | async-start | bytes 1048576 | tf_op jit(solution)/shard_map/psum | solution.py:205
  31.8 3.8 copy-start.11
  35.6 4.0 copy-start.4
  35.6 6.9 %copy-start.3 = (s32[128,8]{0,1:T(8,128)S(1)}, s32[128,8]{0,1:T(8,128)}, u32[]{:S(2)}) copy-start(s32[128,8]{0,1:T(8,128)} %param.31) | copy-start | bytes 12292
  39.6 55.7 %copy-start.5 = (f32[2048]{0:T(1024)S(1)}, f32[2048]{0:T(1024)}, u32[]{:S(2)}) copy-start(f32[2048]{0:T(1024)} %param.30) | copy-start | bytes 24580
  118.1 202.3 %copy-start.12 = (bf16[2,2048,192]{1,2,0:T(8,128)(2,1)S(1)}, bf16[2,2048,192]{1,2,0:T(8,128)(2,1)}, u32[]{:S(2)}) copy-start(bf16[2,2048,192]{1,2,0:T(8,128)(2,1)} %param.33) | copy-start | bytes 4718596
  317.1 3.3 copy-start.2
  354.4 6.2 %copy-start.7 = (f32[128,8]{0,1:T(8,128)S(1)}, f32[128,8]{0,1:T(8,128)}, u32[]{:S(2)}) copy-start(f32[128,8]{0,1:T(8,128)} %param.32) | copy-start | bytes 12292
  354.4 191.9 %all-to-all-start.1 = ((bf16[128,12,2048]{2,1,0:T(8,128)(2,1)}), bf16[128,12,2048]{2,1,0:T(8,128)(2,1)}, u32[]{:S(2)}, u32[]{:S(2)}) async-start(bf16[128,12,2048]{2,1,0:T(8,128)(2,1)} %bitcast.139), calls=%async_computation.1 | async-start | bytes 16777216 | tf_op jit(solution)/shard_map/all_to_all | solution.py:216
  360.6 234.5 %reduce-scatter.2.cloned.1.call-start = ((), (), s32[]{:S(2)}) async-start(), calls=%async_computation.4 | async-start | bytes 655360 | tf_op jit(solution)/shard_map/reduce_scatter | solution.py:218
  557.2 39.5 %copy-start.1 = (bf16[512,2048]{1,0:T(8,128)(2,1)S(1)}, bf16[512,2048]{1,0:T(8,128)(2,1)}, u32[]{:S(2)}) copy-start(bf16[512,2048]{1,0:T(8,128)(2,1)} %param.25) | copy-start | bytes 6291460
Sparse Core Ops, SparseCore 0:
  42.6 50.4 all-reduce.1
  577.3 17.6 reduce-scatter.1
where the time goes:
time: 609 us; the launch traced here: 604 us
  waiting for transfers between devices  253 us (42%)
  blocking collectives  212 us (35%)
  local copies, waits for them, and re-layouts  59 us (10%)
  matrix products  39.3 us (6%)
  other arithmetic  20.7 us (3%)
  between operations  14 us (2%)
  starting transfers between devices  6.23 us (1%)
    all_to_all x1, blocking collectives, body(): lax.all_to_all(send_buffer, 'req', split_axis=0, concat_axis=0, tiled=True)  199 us
    all_to_all x1, waiting for transfers between devices, body(): lax.all_to_all(part_sums, 'req', split_axis=0, concat_axis=0, tiled=True)  186 us
    psum x1, waiting for transfers between devices, body(): lax.psum(head_part.astype(jnp.bfloat16), 'tp').astype(jnp.float32)  49.2 us
    reduce_scatter x1, waiting for transfers between devices, body(): lax.psum_scatter(moe_term.astype(jnp.bfloat16), 'tp', scatter_dimension=1...  17.8 us
    dot_general x1, matrix products, expert_apply(): jnp.einsum('sekf,efd->sekd', hidden_act, down_weight, preferred_element_t...  16.3 us
    all_gather x1, blocking collectives, body(): x_full = lax.all_gather(hidden_in, 'tp', axis=1, tiled=True)  12.9 us
    gather x1, local copies, waits for them, and re-layouts, weigh_back(): returned.reshape(returned.shape[0] * returned.shape[1], row_width)  12.6 us
  transfers between devices with their start and end apart: 3, of which 3 were waited for; matrix products, arithmetic and copies ran while one was open for 0% of the time, Pallas kernels for 0%

commit v1 on v0

v1 whole, which is shorter than its diff:
```python
import functools
import math

import jax
import jax.numpy as jnp
import numpy as np
from jax import lax
from jax.experimental import pallas as pl
from jax.experimental.pallas import tpu as pltpu
from jax.sharding import PartitionSpec as P

PAGE = 128
MAXPG = 32
PRE = 120
TOK = 128
REQS_DEV = 9
POOL = 48
CAP = 12
NORM_EPS = 1e-06
ROPE_BASE = 1000000.0

MESH = pl.DeviceIdType.MESH
F32 = jnp.float32
BF16 = jnp.bfloat16
BLK = 48
CHUNK = 512


def token_layout(lengths):
    local_idx = jnp.arange(TOK, dtype=jnp.int32)
    requests = jnp.where(local_idx < PRE, 0, local_idx - PRE + 1)
    offsets = jnp.where(local_idx < PRE, local_idx, 0)
    request_hot = (requests[:, None] == jnp.arange(REQS_DEV, dtype=jnp.int32)[None, :]).astype(
        jnp.int32
    )
    return jnp.sum(request_hot * lengths[None, :], axis=1) + offsets


def page_slots(table, lengths):
    pages_used = (lengths + PAGE - 1) // PAGE
    entry_live = jnp.arange(MAXPG, dtype=jnp.int32)[None, :] < pages_used[:, None]
    page_match = (
        (table[:, :, None] == jnp.arange(POOL, dtype=jnp.int32)[None, None, :])
        & entry_live[:, :, None]
    ).astype(jnp.int32)
    page_owner = jnp.sum(
        page_match * jnp.arange(REQS_DEV, dtype=jnp.int32)[:, None, None], axis=(0, 1)
    )
    page_start = jnp.sum(
        page_match * (jnp.arange(MAXPG, dtype=jnp.int32) * PAGE)[None, :, None], axis=(0, 1)
    )
    page_used = jnp.sum(page_match, axis=(0, 1)) > 0
    owner_length = jnp.sum(page_match * lengths[:, None, None], axis=(0, 1))
    slot_pos = page_start[:, None] + jnp.arange(PAGE, dtype=jnp.int32)[None, :]
    slot_live = page_used[:, None] & (slot_pos < owner_length[:, None])
    return jnp.where(slot_live, page_owner[:, None], -1)


def rope_tables(positions, head_dim):
    half = head_dim // 2
    exponent = jnp.arange(half, dtype=F32) * (2.0 / head_dim)
    frequency = jnp.power(F32(ROPE_BASE), -exponent)
    angles = positions.astype(F32)[:, None] * frequency[None, :]
    cosine, sine = jnp.cos(angles), jnp.sin(angles)
    return (
        jnp.concatenate([cosine, cosine], axis=1),
        jnp.concatenate([-sine, sine], axis=1),
    )


def mm(a, b):
    return jnp.dot(a, b, preferred_element_type=F32)


def mm_t(a, b):
    return lax.dot_general(a, b, (((1,), (1,)), ((), ())), preferred_element_type=F32)


def iota(shape, dim):
    return lax.broadcasted_iota(jnp.int32, shape, dim)


def layer_kernel(
    nx, nz,
    hid, gin, qgain, kgain, gpost, cos_t, sin_t, owner, ids_t, ids, rw,
    exp_t, slot_t, exp_r, slot_r, perm1, perm2,
    qw, kw, vw, ow, kp, vp, wg_in, wu_in, wd_in,
    out,
    xbuf, nbuf, qw_v, kw_v, vw_v, ow_v, kc, vc, q2, kn, vn, abuf,
    rs_send, rs_recv, st_send, st_recv, nb, resid, s_mat, w_hi, w_lo,
    send1, recv1, zbuf, xe, wg, wu, wd, ye, send2, recv2,
    loc_s, ag_s, ag_r, rs_s, rs_r, st_s, st_r, d1_s, d1_r, d2_s, d2_r, w_s, w_r, f_s,
):
    me_r = lax.axis_index("req")
    my = lax.axis_index("tp")
    core = lax.rem(me_r, 2)
    chip = me_r // 2
    cx = chip // nz
    cz = lax.rem(chip, nz)
    world = chip * 4 + my
    n_world = nx * nz * 4
    n_rows = n_world * CAP
    src_slot = cz * nx + cx

    def peer(k):
        return lax.rem(my + k, 4)

    barrier = pltpu.get_barrier_semaphore()

    def greet(k, carry):
        other = lax.rem(world + k, n_world)
        pl.semaphore_signal(
            barrier, inc=1,
            device_id={"req": (other // 4) * 2 + core, "tp": lax.rem(other, 4)},
            device_id_type=MESH,
        )
        return carry

    lax.fori_loop(1, n_world, greet, 0)
    sibling = {"req": chip * 2 + 1 - core, "tp": my}
    pl.semaphore_signal(barrier, inc=1, device_id=sibling, device_id_type=MESH)

    loads = [
        pltpu.make_async_copy(s, d, loc_s.at[i])
        for i, (s, d) in enumerate(
            [(qw, qw_v), (kw, kw_v), (vw, vw_v), (kp, kc), (vp, vc), (ow, ow_v)]
        )
    ]
    for load in loads:
        load.start()
    xbuf[my] = hid[...]

    lane = iota((TOK, TOK), 1)
    sub = iota((TOK, TOK), 0)
    named_t = jnp.zeros((TOK, TOK), F32)
    named = jnp.zeros((TOK, TOK), F32)
    dense_w = jnp.zeros((TOK, TOK), F32)
    for k in range(8):
        named_t = named_t + (ids_t[k : k + 1, :] == sub).astype(F32)
        hit = (ids[:, k : k + 1] == lane).astype(F32)
        named = named + hit
        dense_w = dense_w + hit * rw[:, k : k + 1]
    before = (sub < lane).astype(BF16)
    after = (lane < sub).astype(BF16)
    rank_t = jnp.where(named_t > 0, mm(named_t.astype(BF16), before), -1.0)
    rank = jnp.where(named > 0, mm(after, named.astype(BF16)), -1.0)
    s_mat[...] = (mm(exp_t[...], rank_t.astype(BF16)) == slot_t[...].astype(F32)).astype(BF16)
    chosen = mm(rank.astype(BF16), exp_r[...]) == slot_r[...]
    dw_hi = dense_w.astype(BF16)
    dw_lo = (dense_w - dw_hi.astype(F32)).astype(BF16)
    w_hi[...] = jnp.where(chosen, mm(dw_hi, exp_r[...]), 0.0).astype(BF16)
    w_lo[...] = jnp.where(chosen, mm(dw_lo, exp_r[...]), 0.0).astype(BF16)

    pl.semaphore_wait(barrier, n_world)

    def ag_copy(k):
        return pltpu.make_async_remote_copy(
            src_ref=hid, dst_ref=xbuf.at[my], send_sem=ag_s.at[k - 1], recv_sem=ag_r.at[k - 1],
            device_id={"tp": peer(k)}, device_id_type=MESH,
        )

    for k in (1, 3, 2):
        ag_copy(k).start()

    w_pairs = ((wg_in, wg), (wu_in, wu), (wd_in, wd))

    def w_remote(a, i):
        return pltpu.make_async_remote_copy(
            src_ref=w_pairs[a][0].at[i], dst_ref=w_pairs[a][1].at[my],
            send_sem=w_s.at[a, i], recv_sem=w_r.at[a, my],
            device_id={"tp": 2 * core + i}, device_id_type=MESH,
        )

    def w_start(a):
        for i in range(2):
            @pl.when(2 * core + i != my)
            def _():
                w_remote(a, i).start()

            @pl.when(2 * core + i == my)
            def _():
                pltpu.make_async_copy(
                    w_pairs[a][0].at[i], w_pairs[a][1].at[my], w_r.at[a, my]
                ).start()

    def w_forward(a, j):
        return pltpu.make_async_remote_copy(
            src_ref=w_pairs[a][1].at[j], dst_ref=w_pairs[a][1].at[j],
            send_sem=f_s.at[a, j], recv_sem=w_r.at[a, j],
            device_id=sibling, device_id_type=MESH,
        )

    def w_wait(a, j):
        ref = w_pairs[a][1].at[j]
        pltpu.make_async_copy(ref, ref, w_r.at[a, j]).wait()

    primary = core == my // 2

    def w_pass_on(a):
        @pl.when(primary)
        def _():
            for j in range(4):
                w_wait(a, j)
                w_forward(a, j).start()

    w_start(0)

    for k in (1, 3, 2):
        ag_copy(k).wait_recv()
    x_all = jnp.concatenate([xbuf[j].astype(F32) for j in range(4)], axis=1)
    mean_sq = jnp.mean(x_all * x_all, axis=-1, keepdims=True)
    nbuf[...] = (x_all * lax.rsqrt(mean_sq + NORM_EPS) * gin[...]).astype(BF16)
    for load in loads[:3]:
        load.wait()

    def head_norm(v, gain):
        ms = jnp.mean(v * v, axis=-1, keepdims=True)
        v = v * lax.rsqrt(ms + NORM_EPS) * gain
        return (v * cos_t[...] + pltpu.roll(v, 64, 1) * sin_t[...]).astype(BF16)

    q_lin = mm(nbuf[...], qw_v[...])
    for g in range(4):
        q2[g * TOK : (g + 1) * TOK, :] = head_norm(q_lin[:, g * 128 : (g + 1) * 128], qgain[...])
    kn[...] = head_norm(mm(nbuf[...], kw_v[...]), kgain[...])
    vn[...] = mm(nbuf[...], vw_v[...]).astype(BF16)

    inv_root = 1.0 / math.sqrt(128)
    n_q = 4 * TOK
    row_tok = lax.rem(iota((n_q, 1), 0), TOK)
    row_req = jnp.where(row_tok < PRE, 0, row_tok - PRE + 1)
    key_tok = iota((n_q, TOK), 1)
    new_mask = (key_tok == row_tok) | ((row_tok < PRE) & (key_tok <= row_tok))
    sc = jnp.where(new_mask, mm_t(q2[...], kn[...]) * inv_root, -1e30)
    m0 = jnp.max(sc, axis=-1, keepdims=True)
    pr = jnp.exp(sc - m0)
    l0 = jnp.sum(pr, axis=-1, keepdims=True)
    acc0 = mm(pr.astype(BF16), vn[...])
    for load in loads[3:5]:
        load.wait()

    def attend_chunk(j, carry):
        m, l, acc = carry
        at = pl.multiple_of(j * CHUNK, CHUNK)
        s = mm_t(q2[...], kc[pl.ds(at, CHUNK), :]) * inv_root
        s = jnp.where(owner[j] == row_req, s, -1e30)
        m_new = jnp.maximum(m, jnp.max(s, axis=-1, keepdims=True))
        scale = jnp.exp(m - m_new)
        p = jnp.exp(s - m_new)
        l = l * scale + jnp.sum(p, axis=-1, keepdims=True)
        acc = acc * scale + mm(p.astype(BF16), vc[pl.ds(at, CHUNK), :])
        return m_new, l, acc

    _, l_all, acc_all = lax.fori_loop(0, POOL * PAGE // CHUNK, attend_chunk, (m0, l0, acc0))
    att = (acc_all / l_all).astype(BF16)
    for g in range(4):
        abuf[:, g * 128 : (g + 1) * 128] = att[g * TOK : (g + 1) * TOK, :]
    loads[5].wait()
    for j in range(4):
        rs_send[j] = mm(abuf[...], ow_v[:, j * 512 : (j + 1) * 512]).astype(BF16)

    def rs_copy(k):
        return pltpu.make_async_remote_copy(
            src_ref=rs_send.at[peer(k)], dst_ref=rs_recv.at[k - 1],
            send_sem=rs_s.at[k - 1], recv_sem=rs_r.at[k - 1],
            device_id={"tp": peer(k)}, device_id_type=MESH,
        )

    for k in (1, 3, 2):
        rs_copy(k).start()
    total = hid[...].astype(F32) + rs_send[my].astype(F32)
    for k in (1, 3, 2):
        rs_copy(k).wait_recv()
        total = total + rs_recv[k - 1].astype(F32)
    resid[...] = total
    col = jnp.sum(total * total, axis=-1, keepdims=True)
    diag = sub == lane
    row = jnp.sum(jnp.where(diag, col, 0.0), axis=0, keepdims=True)
    st_send[...] = jnp.broadcast_to(row, (8, TOK))

    def st_copy(k):
        return pltpu.make_async_remote_copy(
            src_ref=st_send, dst_ref=st_recv.at[k - 1],
            send_sem=st_s.at[k - 1], recv_sem=st_r.at[k - 1],
            device_id={"tp": peer(k)}, device_id_type=MESH,
        )

    for k in (1, 3, 2):
        st_copy(k).start()
    w_start(1)
    w_start(2)
    for k in (1, 3, 2):
        st_copy(k).wait_recv()
    row = st_send[0:1, :] + st_recv[0, 0:1, :] + st_recv[1, 0:1, :] + st_recv[2, 0:1, :]
    col = jnp.sum(jnp.where(diag, row, 0.0), axis=-1, keepdims=True)
    nb[...] = (
        resid[...] * lax.rsqrt(col * (1.0 / 2048.0) + NORM_EPS) * gpost[my]
    ).astype(BF16)

    def dz_of(jj):
        return lax.rem(nz // 2 + ((jj + 1) // 2) * (1 - 2 * lax.rem(jj, 2)) + nz, nz)

    def chip_at(jj, dx):
        return lax.rem(cx + dx, nx), lax.rem(cz + dz_of(jj), nz)

    def d1_copy(jj, dx, k, local=False):
        gx, gz = chip_at(jj, dx)
        g = gx * nz + gz
        src = send1.at[pl.ds(pl.multiple_of((g * 4 + peer(k)) * BLK, 16), BLK)]
        dst = recv1.at[my, pl.ds(pl.multiple_of(src_slot * BLK, 16), BLK)]
        if local:
            return pltpu.make_async_copy(src, dst, d1_r.at[jj])
        return pltpu.make_async_remote_copy(
            src_ref=src, dst_ref=dst, send_sem=d1_s, recv_sem=d1_r.at[jj],
            device_id={"req": g * 2 + core, "tp": peer(k)}, device_id_type=MESH,
        )

    def d2_copy(jj, dx, k, local=False):
        gx, gz = chip_at(jj, dx)
        src = send2.at[peer(k), pl.ds(pl.multiple_of((gz * nx + gx) * BLK, 16), BLK)]
        dst = recv2.at[pl.ds(pl.multiple_of(world * BLK, 16), BLK)]
        if local:
            return pltpu.make_async_copy(src, dst, d2_r.at[jj])
        return pltpu.make_async_remote_copy(
            src_ref=src, dst_ref=dst, send_sem=d2_s, recv_sem=d2_r.at[jj],
            device_id={"req": (gx * nz + gz) * 2 + core, "tp": peer(k)}, device_id_type=MESH,
        )

    def send_all(copy_of, jj, last=False):
        for dx in range(nx):
            for k in range(4):
                copy_of(jj, dx, k, local=last and dx == 0 and k == 0).start()

    def build(jj):
        parts = []
        for dx in range(nx):
            gx, gz = chip_at(jj, dx)
            at = pl.multiple_of((gx * nz + gz) * BLK, 16)
            z = mm(s_mat[pl.ds(at, BLK), :], nb[...]).astype(BF16)
            parts.append(jnp.concatenate([z[:, i * 128 : (i + 1) * 128] for i in range(4)], axis=0))
        o = mm(perm2[...], jnp.concatenate(parts, axis=1)).astype(BF16)
        for dx in range(nx):
            gx, gz = chip_at(jj, dx)
            at = pl.multiple_of((gx * nz + gz) * 4 * BLK, 16)
            send1[pl.ds(at, 4 * BLK), :] = o[:, dx * 128 : (dx + 1) * 128]

    build(0)

    def build_step(jj, carry):
        build(jj)
        send_all(d1_copy, jj - 1)
        return carry

    lax.fori_loop(1, nz, build_step, 0)
    send_all(d1_copy, nz - 1, last=True)

    w_pass_on(0)
    w_pass_on(1)
    w_pass_on(2)

    def d_wait(ref, sem):
        pltpu.make_async_copy(ref, ref, sem).wait()

    for jj in range(nz):
        d_wait(recv1.at[0, pl.ds(0, 4 * nx * BLK)], d1_r.at[jj])

    def unpack(gz, carry):
        at = pl.multiple_of(gz * nx * BLK, 16)
        x = jnp.concatenate([recv1[q, pl.ds(at, nx * BLK), :] for q in range(4)], axis=1)
        o = mm(perm1[...], x).astype(BF16)
        to = pl.multiple_of(gz * BLK, 16)
        for q in range(4):
            for i in range(4):
                xe[pl.ds(to, BLK), (q * 4 + i) * 128 : (q * 4 + i + 1) * 128] = o[
                    i * BLK : (i + 1) * BLK, q * 128 : (q + 1) * 128
                ]
        return carry

    lax.fori_loop(0, nz, unpack, 0)

    @pl.when(jnp.logical_not(primary))
    def _():
        for a in range(3):
            for j in range(4):
                w_wait(a, j)

    half_rows = nx * nz * CAP // 2
    ye[...] = jnp.zeros_like(ye)

    def expert_step(t, carry):
        j = t // 2
        rows = pl.ds(pl.multiple_of(lax.rem(t, 2) * half_rows, 16), half_rows)
        x = xe[rows, :]
        gate = mm(x, wg[j])
        up = mm(x, wu[j])
        act = (gate / (1.0 + jnp.exp(-gate)) * up).astype(BF16)
        ye[rows, :] += mm(act, wd[j])
        return carry

    lax.fori_loop(0, 8, expert_step, 0)

    def pack(jj):
        gz = lax.rem(cz + dz_of(jj), nz)
        rows = pl.ds(pl.multiple_of(gz * BLK, 16), BLK)
        parts = []
        for i in range(4):
            parts.append(
                jnp.concatenate(
                    [ye[rows, (q * 4 + i) * 128 : (q * 4 + i + 1) * 128] for q in range(4)], axis=1
                ).astype(BF16)
            )
        o = mm(perm2[...], jnp.concatenate(parts, axis=0)).astype(BF16)
        at = pl.multiple_of(gz * nx * BLK, 16)
        for q in range(4):
            send2[q, pl.ds(at, nx * BLK), :] = o[:, q * 128 : (q + 1) * 128]

    pack(0)

    def pack_step(jj, carry):
        pack(jj)
        send_all(d2_copy, jj - 1)
        return carry

    lax.fori_loop(1, nz, pack_step, 0)
    send_all(d2_copy, nz - 1, last=True)

    for jj in range(nz):
        d_wait(recv2.at[pl.ds(0, 4 * nx * BLK)], d2_r.at[jj])

    def collect(b, carry):
        x = jnp.concatenate(
            [recv2[pl.ds(pl.multiple_of((b * 4 + i) * 4 * BLK, 16), 4 * BLK), :] for i in range(4)],
            axis=1,
        )
        o = mm(perm1[...], x).astype(BF16)
        for i in range(4):
            to = pl.multiple_of((b * 4 + i) * BLK, 16)
            for q in range(4):
                zbuf[pl.ds(to, BLK), q * 128 : (q + 1) * 128] = o[
                    q * BLK : (q + 1) * BLK, i * 128 : (i + 1) * 128
                ]
        return carry

    lax.fori_loop(0, nx * nz // 4, collect, 0)
    moe = mm(w_hi[...], zbuf[...]) + mm(w_lo[...], zbuf[...])
    out[...] = (resid[...] + moe).astype(BF16)

    for k in (1, 2, 3):
        ag_copy(k).wait_send()
        rs_copy(k).wait_send()
        st_copy(k).wait_send()
    for a in range(3):
        for i in range(2):
            @pl.when(2 * core + i != my)
            def _():
                w_remote(a, i).wait_send()

    @pl.when(primary)
    def _():
        for a in range(3):
            for j in range(4):
                w_forward(a, j).wait_send()

    sent = pl.ds(0, (n_world - 1) * BLK)
    d_wait(send1.at[sent], d1_s)
    d_wait(recv2.at[sent], d2_s)


def perm_tables():
    index = np.arange(4 * BLK)
    l, b, c = index // BLK, (index % BLK) // CAP, index % CAP
    table = np.zeros((4 * BLK, 4 * BLK), np.float32)
    table[index, b * BLK + l * CAP + c] = 1.0
    return table, table.T.copy()


def body(
    nx, nz,
    hidden_in, norm_in_gain, q_weight, k_weight, v_weight, q_gain, k_gain, o_weight,
    key_pages, value_pages, page_table, cache_len, norm_post_gain, expert_ids, route_weights,
    gate_weight, up_weight, down_weight,
):
    n_chip = nx * nz
    n_world = n_chip * 4
    n_rows = n_world * CAP
    width = hidden_in.shape[1]
    model = norm_in_gain.shape[0]
    ff = gate_weight.shape[2]
    cos_t, sin_t = rope_tables(token_layout(cache_len), 128)
    owner = page_slots(page_table, cache_len).reshape(POOL * PAGE // CHUNK, 1, CHUNK)
    slots = np.arange(n_rows)
    exp_t = (slots[:, None] // CAP == np.arange(TOK)[None, :]).astype(np.float32)
    slot_t = np.broadcast_to((slots % CAP)[:, None], (n_rows, TOK)).astype(np.float32)
    p1, p2 = perm_tables()
    small = [
        hidden_in, norm_in_gain[None, :], q_gain[None, :], k_gain[None, :],
        norm_post_gain.reshape(4, 1, width), cos_t, sin_t, owner,
        expert_ids.T, expert_ids, route_weights,
        jnp.asarray(exp_t, BF16), jnp.asarray(slot_t, BF16), jnp.asarray(exp_t.T, BF16),
        jnp.asarray((slots % CAP)[None, :], F32), jnp.asarray(p1, BF16), jnp.asarray(p2, BF16),
    ]
    cache = POOL * PAGE
    large = [
        q_weight, k_weight, v_weight, o_weight,
        key_pages.reshape(cache, 128), value_pages.reshape(cache, 128),
        gate_weight, up_weight, down_weight,
    ]
    vmem = lambda shape, dtype=BF16: pltpu.VMEM(shape, dtype)
    dma = pltpu.SemaphoreType.DMA
    rows = n_chip * CAP
    return pl.pallas_call(
        functools.partial(layer_kernel, nx, nz),
        out_shape=jax.ShapeDtypeStruct((TOK, width), BF16),
        in_specs=[pl.BlockSpec(memory_space=pltpu.VMEM)] * len(small)
        + [pl.BlockSpec(memory_space=pl.ANY)] * len(large),
        out_specs=pl.BlockSpec(memory_space=pltpu.VMEM),
        scratch_shapes=[
            vmem((4, TOK, width)), vmem((TOK, model)),
            vmem(q_weight.shape), vmem(k_weight.shape), vmem(v_weight.shape), vmem(o_weight.shape),
            vmem((cache, 128)), vmem((cache, 128)),
            vmem((4 * TOK, 128)), vmem((TOK, 128)), vmem((TOK, 128)), vmem((TOK, 512)),
            vmem((4, TOK, width)), vmem((3, TOK, width)),
            vmem((8, TOK), F32), vmem((3, 8, TOK), F32),
            vmem((TOK, width)), vmem((TOK, width), F32),
            vmem((n_rows, TOK)), vmem((TOK, n_rows)), vmem((TOK, n_rows)),
            vmem((n_world * BLK, 128)), vmem((4, n_chip * BLK, 128)),
            vmem((n_rows, width)), vmem((rows, model)),
            vmem((4, model, ff)), vmem((4, model, ff)), vmem((4, ff, model)),
            vmem((rows, model), F32),
            vmem((4, n_chip * BLK, 128)), vmem((n_world * BLK, 128)),
            dma((6,)), dma((3,)), dma((3,)), dma((3,)), dma((3,)), dma((3,)), dma((3,)),
            dma, dma((nz,)), dma, dma((nz,)), dma((3, 2)), dma((3, 4)), dma((3, 4)),
        ],
        compiler_params=pltpu.CompilerParams(
            collective_id=0, has_side_effects=True, vmem_limit_bytes=62 * 1024 * 1024
        ),
    )(*small, *large)


def solution(mesh):
    nx = 4
    nz = mesh.shape["req"] // (2 * nx)
    return jax.shard_map(
        functools.partial(body, nx, nz),
        mesh=mesh,
        in_specs=(
            P("req", "tp"), P(), P(None, "tp"), P(None, "tp"), P(None, "tp"), P(), P(),
            P("tp", None), P("tp", "req", None, None), P("tp", "req", None, None),
            P("req", None), P("req"), P(), P("req", None), P("req", None),
            P("req", None, "tp"), P("req", None, "tp"), P("req", "tp", None),
        ),
        out_specs=P("req", "tp"),
        check_vma=False,
    )
```

time: 609 us -> 178 us (0.29)
  waiting for transfers between devices: 253 us -> 0 us
  blocking collectives: 212 us -> 0 us
  Pallas kernels: 0 us -> 163 us
  local copies, waits for them, and re-layouts: 59 us -> 11.3 us
  matrix products: 39.3 us -> 0 us
  other arithmetic: 20.7 us -> 4.1 us
  between operations: 14 us -> 0.06 us
  starting transfers between devices: 6.23 us -> 0 us
    all_to_all x1 -> x0, blocking collectives: 199 us -> none  [body(): lax.all_to_all(send_buffer, 'req', split_axis=0, concat_axis=0, tiled=True)]
    all_to_all x1 -> x0, waiting for transfers between devices: 186 us -> none  [body(): lax.all_to_all(part_sums, 'req', split_axis=0, concat_axis=0, tiled=True)]
    pallas_call x0 -> x1, Pallas kernels: none -> 163 us  [body(): pl.pallas_call(functools.partial(layer_kernel, nx, nz), out_shape=jax.Sha...]
    psum x1 -> x0, waiting for transfers between devices: 49.2 us -> none  [body(): lax.psum(head_part.astype(jnp.bfloat16), 'tp').astype(jnp.float32)]
    dot_general x9 -> x0, matrix products: 39.3 us -> none  [the longest x1 16.3 us: expert_apply(): jnp.einsum('sekf,efd->sekd', hidden_act, down_weight, preferred_element_t...]
    reshape x4 -> x0, local copies, waits for them, and re-layouts: 31.4 us -> none  [the longest x1 10.9 us: weigh_back(): returned.reshape(returned.shape[0] * returned.shape[1], row_width)]
    reduce_scatter x1 -> x0, waiting for transfers between devices: 17.8 us -> none  [body(): lax.psum_scatter(moe_term.astype(jnp.bfloat16), 'tp', scatter_dimension=1...]
    all_gather x1 -> x0, blocking collectives: 12.9 us -> none  [body(): x_full = lax.all_gather(hidden_in, 'tp', axis=1, tiled=True)]
  transfers between devices with their start and end apart: 3 -> 0, of which waited for: 3 -> 0; matrix products, arithmetic and copies ran while one was open for 0% -> 0% of each run, Pallas kernels for 0% -> 0%
where the time goes in v1:
time: 178 us
  Pallas kernels  163 us (92%)
  local copies, waits for them, and re-layouts  11.3 us (6%)
  other arithmetic  4.1 us (2%)
    pallas_call x1, Pallas kernels, body(): pl.pallas_call(functools.partial(layer_kernel, nx, nz), out_shape=jax.Sha...  163 us
    unnamed x7, local copies, waits for them, and re-layouts  10.6 us

profile of v1, /device:TPU:1, one launch (start us, length us, event | category | flops | bytes accessed | tf_op | source)
XLA Modules:
  0.0 178.1 jit_solution(5756688305735384322)
XLA Ops:
  0.0 0.7 and_select_fusion.1
  0.7 0.7 select_reduce_fusion.3
  1.4 0.1 iota_compare_fusion.1
  1.5 0.9 select_reduce_fusion.2
  2.4 0.1 gt.15
  2.5 0.1 and.33
  2.6 0.1 add.57
  2.7 0.1 broadcast_in_dim.32
  2.7 0.1 lt.53
  2.8 0.1 lt.54
  2.9 0.1 broadcast_in_dim.54
  3.0 0.1 add.58
  3.1 0.7 and_select_fusion.owner
  3.8 1.4 copy.36.rw
  5.2 1.4 copy.35.ids
  6.6 0.3 fusion.1
  6.9 0.7 pad_maximum_fusion
  7.6 0.0 copy-start
  7.6 3.8 %copy.37.wg_in = bf16[2,2048,192]{2,1,0:T(8,128)(2,1)} copy(bf16[2,2048,192]{1,2,0:T(8,128)(2,1)} %param.39) | data formatting | bytes 3145728 | tf_op args[15]
  11.5 0.0 copy-done
  11.5 2.4 %copy.38.wu_in = bf16[2,2048,192]{2,1,0:T(8,128)(2,1)} copy(bf16[2,2048,192]{1,2,0:T(8,128)(2,1)S(1)} %copy-done) | data formatting | bytes 3145728 | tf_op args[16]
  13.9 162.7 %shard_map.226 = bf16[128,512]{1,0:T(8,128)(2,1)} custom-call(bf16[128,512]{1,0:T(8,128)(2,1)} %hid.1, f32[1,2048]{1,0:T(1,128)} %bitcast.18, f32[1,128]{1,0:T(1,128)} %bitcast.20, f32[1,128]{1,0:T(1,128)} %bitcast.21, f32[4,1,512]{2,1,0:T(1,128)} %bitcast.19, f32[128,128]{1,0:T(8,128)} %get-tuple-element.12.cos_t, f32[128,128]{1,0:T(8,128)} %get-tuple-element.13.sin_t, ...), custom_call_target="tpu_custom_call" | custom-call | tf_op jit(solution)/shard_map/pallas_call | solution.py:510
  176.5 1.6 copy.40
  (7 shorter events, 0.1 us)
Async XLA Ops:
  7.6 3.8 %copy-start = (bf16[2,2048,192]{1,2,0:T(8,128)(2,1)S(1)}, bf16[2,2048,192]{1,2,0:T(8,128)(2,1)}, u32[]{:S(2)}) copy-start(bf16[2,2048,192]{1,2,0:T(8,128)(2,1)} %param.40) | copy-start | bytes 4718596

commit v2 on v1

--- a/solution.py
+++ b/solution.py
@@ -26,48 +26,6 @@
 CHUNK = 512
 
 
-def token_layout(lengths):
-    local_idx = jnp.arange(TOK, dtype=jnp.int32)
-    requests = jnp.where(local_idx < PRE, 0, local_idx - PRE + 1)
-    offsets = jnp.where(local_idx < PRE, local_idx, 0)
-    request_hot = (requests[:, None] == jnp.arange(REQS_DEV, dtype=jnp.int32)[None, :]).astype(
-        jnp.int32
-    )
-    return jnp.sum(request_hot * lengths[None, :], axis=1) + offsets
-
-
-def page_slots(table, lengths):
-    pages_used = (lengths + PAGE - 1) // PAGE
-    entry_live = jnp.arange(MAXPG, dtype=jnp.int32)[None, :] < pages_used[:, None]
-    page_match = (
-        (table[:, :, None] == jnp.arange(POOL, dtype=jnp.int32)[None, None, :])
-        & entry_live[:, :, None]
-    ).astype(jnp.int32)
-    page_owner = jnp.sum(
-        page_match * jnp.arange(REQS_DEV, dtype=jnp.int32)[:, None, None], axis=(0, 1)
-    )
-    page_start = jnp.sum(
-        page_match * (jnp.arange(MAXPG, dtype=jnp.int32) * PAGE)[None, :, None], axis=(0, 1)
-    )
-    page_used = jnp.sum(page_match, axis=(0, 1)) > 0
-    owner_length = jnp.sum(page_match * lengths[:, None, None], axis=(0, 1))
-    slot_pos = page_start[:, None] + jnp.arange(PAGE, dtype=jnp.int32)[None, :]
-    slot_live = page_used[:, None] & (slot_pos < owner_length[:, None])
-    return jnp.where(slot_live, page_owner[:, None], -1)
-
-
-def rope_tables(positions, head_dim):
-    half = head_dim // 2
-    exponent = jnp.arange(half, dtype=F32) * (2.0 / head_dim)
-    frequency = jnp.power(F32(ROPE_BASE), -exponent)
-    angles = positions.astype(F32)[:, None] * frequency[None, :]
-    cosine, sine = jnp.cos(angles), jnp.sin(angles)
-    return (
-        jnp.concatenate([cosine, cosine], axis=1),
-        jnp.concatenate([-sine, sine], axis=1),
-    )
-
-
 def mm(a, b):
     return jnp.dot(a, b, preferred_element_type=F32)
 
@@ -82,11 +40,11 @@
 
 def layer_kernel(
     nx, nz,
-    hid, gin, qgain, kgain, gpost, cos_t, sin_t, owner, ids_t, ids, rw,
+    lens, hid, gin, qgain, kgain, gpost, freq, table, ids_t, rw_t,
     exp_t, slot_t, exp_r, slot_r, perm1, perm2,
     qw, kw, vw, ow, kp, vp, wg_in, wu_in, wd_in,
     out,
-    xbuf, nbuf, qw_v, kw_v, vw_v, ow_v, kc, vc, q2, kn, vn, abuf,
+    owner, cos_t, sin_t, xbuf, nbuf, qw_v, kw_v, vw_v, ow_v, kc, vc, q2, kn, vn, abuf,
     rs_send, rs_recv, st_send, st_recv, nb, resid, s_mat, w_hi, w_lo,
     send1, recv1, zbuf, xe, wg, wu, wd, ye, send2, recv2,
     loc_s, ag_s, ag_r, rs_s, rs_r, st_s, st_r, d1_s, d1_r, d2_s, d2_r, w_s, w_r, f_s,
@@ -133,23 +91,47 @@
     lane = iota((TOK, TOK), 1)
     sub = iota((TOK, TOK), 0)
     named_t = jnp.zeros((TOK, TOK), F32)
-    named = jnp.zeros((TOK, TOK), F32)
-    dense_w = jnp.zeros((TOK, TOK), F32)
+    dense_t = jnp.zeros((TOK, TOK), F32)
     for k in range(8):
-        named_t = named_t + (ids_t[k : k + 1, :] == sub).astype(F32)
-        hit = (ids[:, k : k + 1] == lane).astype(F32)
-        named = named + hit
-        dense_w = dense_w + hit * rw[:, k : k + 1]
+        hit = (ids_t[k : k + 1, :] == sub).astype(F32)
+        named_t = named_t + hit
+        dense_t = dense_t + hit * rw_t[k : k + 1, :]
     before = (sub < lane).astype(BF16)
-    after = (lane < sub).astype(BF16)
     rank_t = jnp.where(named_t > 0, mm(named_t.astype(BF16), before), -1.0)
-    rank = jnp.where(named > 0, mm(after, named.astype(BF16)), -1.0)
     s_mat[...] = (mm(exp_t[...], rank_t.astype(BF16)) == slot_t[...].astype(F32)).astype(BF16)
-    chosen = mm(rank.astype(BF16), exp_r[...]) == slot_r[...]
+    chosen = mm(rank_t.T.astype(BF16), exp_r[...]) == slot_r[...]
+    dense_w = dense_t.T
     dw_hi = dense_w.astype(BF16)
     dw_lo = (dense_w - dw_hi.astype(F32)).astype(BF16)
     w_hi[...] = jnp.where(chosen, mm(dw_hi, exp_r[...]), 0.0).astype(BF16)
     w_lo[...] = jnp.where(chosen, mm(dw_lo, exp_r[...]), 0.0).astype(BF16)
+
+    page = iota((POOL, MAXPG), 0)
+    entry = iota((POOL, MAXPG), 1)
+    own_sum = jnp.zeros((POOL, MAXPG), jnp.int32)
+    start_sum = jnp.zeros((POOL, MAXPG), jnp.int32)
+    len_sum = jnp.zeros((POOL, MAXPG), jnp.int32)
+    tok_col = iota((TOK, 64), 0)
+    tok_req = jnp.where(tok_col < PRE, 0, tok_col - PRE + 1)
+    position = jnp.where(tok_col < PRE, tok_col, 0)
+    for r in range(REQS_DEV):
+        length = lens[r]
+        match = (table[r : r + 1, :] == page) & (entry * PAGE < length)
+        own_sum = own_sum + jnp.where(match, r + 1, 0)
+        start_sum = start_sum + jnp.where(match, entry * PAGE, 0)
+        len_sum = len_sum + jnp.where(match, length, 0)
+        position = position + jnp.where(tok_req == r, length, 0)
+
+    def lane_sum(v):
+        return jnp.sum(v.astype(F32), axis=1, keepdims=True).astype(jnp.int32)
+
+    slot_pos = lane_sum(start_sum) + iota((POOL, PAGE), 1)
+    own_col = lane_sum(own_sum)
+    owner[...] = jnp.where((own_col > 0) & (slot_pos < lane_sum(len_sum)), own_col - 1, -1)
+    angle = position.astype(F32) * freq[...]
+    cosine, sine = jnp.cos(angle), jnp.sin(angle)
+    cos_t[...] = jnp.concatenate([cosine, cosine], axis=1)
+    sin_t[...] = jnp.concatenate([-sine, sine], axis=1)
 
     pl.semaphore_wait(barrier, n_world)
 
@@ -242,7 +224,10 @@
         m, l, acc = carry
         at = pl.multiple_of(j * CHUNK, CHUNK)
         s = mm_t(q2[...], kc[pl.ds(at, CHUNK), :]) * inv_root
-        s = jnp.where(owner[j] == row_req, s, -1e30)
+        own = jnp.concatenate(
+            [owner[pl.ds(j * (CHUNK // PAGE) + i, 1), :] for i in range(CHUNK // PAGE)], axis=1
+        )
+        s = jnp.where(own == row_req, s, -1e30)
         m_new = jnp.maximum(m, jnp.max(s, axis=-1, keepdims=True))
         scale = jnp.exp(m - m_new)
         p = jnp.exp(s - m_new)
@@ -390,8 +375,8 @@
         j = t // 2
         rows = pl.ds(pl.multiple_of(lax.rem(t, 2) * half_rows, 16), half_rows)
         x = xe[rows, :]
-        gate = mm(x, wg[j])
-        up = mm(x, wu[j])
+        gate = mm_t(x, wg[j])
+        up = mm_t(x, wu[j])
         act = (gate / (1.0 + jnp.exp(-gate)) * up).astype(BF16)
         ye[rows, :] += mm(act, wd[j])
         return carry
@@ -485,16 +470,16 @@
     width = hidden_in.shape[1]
     model = norm_in_gain.shape[0]
     ff = gate_weight.shape[2]
-    cos_t, sin_t = rope_tables(token_layout(cache_len), 128)
-    owner = page_slots(page_table, cache_len).reshape(POOL * PAGE // CHUNK, 1, CHUNK)
+    half = np.arange(64, dtype=np.float64)
+    freq = np.power(ROPE_BASE, -2.0 * half / 128.0)
     slots = np.arange(n_rows)
     exp_t = (slots[:, None] // CAP == np.arange(TOK)[None, :]).astype(np.float32)
     slot_t = np.broadcast_to((slots % CAP)[:, None], (n_rows, TOK)).astype(np.float32)
     p1, p2 = perm_tables()
     small = [
         hidden_in, norm_in_gain[None, :], q_gain[None, :], k_gain[None, :],
-        norm_post_gain.reshape(4, 1, width), cos_t, sin_t, owner,
-        expert_ids.T, expert_ids, route_weights,
+        norm_post_gain.reshape(4, 1, width), jnp.asarray(freq[None, :], F32), page_table,
+        expert_ids.T, route_weights.T,
         jnp.asarray(exp_t, BF16), jnp.asarray(slot_t, BF16), jnp.asarray(exp_t.T, BF16),
         jnp.asarray((slots % CAP)[None, :], F32), jnp.asarray(p1, BF16), jnp.asarray(p2, BF16),
     ]
@@ -502,7 +487,7 @@
     large = [
         q_weight, k_weight, v_weight, o_weight,
         key_pages.reshape(cache, 128), value_pages.reshape(cache, 128),
-        gate_weight, up_weight, down_weight,
+        jnp.swapaxes(gate_weight, 1, 2), jnp.swapaxes(up_weight, 1, 2), down_weight,
     ]
     vmem = lambda shape, dtype=BF16: pltpu.VMEM(shape, dtype)
     dma = pltpu.SemaphoreType.DMA
@@ -510,10 +495,12 @@
     return pl.pallas_call(
         functools.partial(layer_kernel, nx, nz),
         out_shape=jax.ShapeDtypeStruct((TOK, width), BF16),
-        in_specs=[pl.BlockSpec(memory_space=pltpu.VMEM)] * len(small)
+        in_specs=[pl.BlockSpec(memory_space=pltpu.SMEM)]
+        + [pl.BlockSpec(memory_space=pltpu.VMEM)] * len(small)
         + [pl.BlockSpec(memory_space=pl.ANY)] * len(large),
         out_specs=pl.BlockSpec(memory_space=pltpu.VMEM),
         scratch_shapes=[
+            vmem((POOL, PAGE), jnp.int32), vmem((TOK, 128), F32), vmem((TOK, 128), F32),
             vmem((4, TOK, width)), vmem((TOK, model)),
             vmem(q_weight.shape), vmem(k_weight.shape), vmem(v_weight.shape), vmem(o_weight.shape),
             vmem((cache, 128)), vmem((cache, 128)),
@@ -524,7 +511,7 @@
             vmem((n_rows, TOK)), vmem((TOK, n_rows)), vmem((TOK, n_rows)),
             vmem((n_world * BLK, 128)), vmem((4, n_chip * BLK, 128)),
             vmem((n_rows, width)), vmem((rows, model)),
-            vmem((4, model, ff)), vmem((4, model, ff)), vmem((4, ff, model)),
+            vmem((4, ff, model)), vmem((4, ff, model)), vmem((4, ff, model)),
             vmem((rows, model), F32),
             vmem((4, n_chip * BLK, 128)), vmem((n_world * BLK, 128)),
             dma((6,)), dma((3,)), dma((3,)), dma((3,)), dma((3,)), dma((3,)), dma((3,)),
@@ -533,7 +520,7 @@
         compiler_params=pltpu.CompilerParams(
             collective_id=0, has_side_effects=True, vmem_limit_bytes=62 * 1024 * 1024
         ),
-    )(*small, *large)
+    )(cache_len, *small, *large)
 
 
 def solution(mesh):

time: 178 us -> 153 us (0.86)
  Pallas kernels: 163 us -> 152 us
  local copies, waits for them, and re-layouts: 11.3 us -> 1.57 us
  other arithmetic: 4.1 us -> 0 us
    pallas_call x1, Pallas kernels: 163 us -> 152 us  [body(): pl.pallas_call(functools.partial(layer_kernel, nx, nz), out_shape=jax.Sha...]
    unnamed x7 -> x1, local copies, waits for them, and re-layouts: 10.6 us -> 1.57 us
where the time goes in v2:
time: 153 us
  Pallas kernels  152 us (99%)
  local copies, waits for them, and re-layouts  1.57 us (1%)
    pallas_call x1, Pallas kernels, body(): pl.pallas_call(functools.partial(layer_kernel, nx, nz), out_shape=jax.Sha...  152 us

profile of v2, /device:TPU:1, one launch (start us, length us, event | category | flops | bytes accessed | tf_op | source)
XLA Modules:
  0.0 153.3 jit_solution(8105032374202386254)
XLA Ops:
  0.0 151.7 %shard_map.235 = bf16[128,512]{1,0:T(8,128)(2,1)} custom-call(s32[9]{0:T(128)} %lens.1, bf16[128,512]{1,0:T(8,128)(2,1)} %hid.1, f32[1,2048]{1,0:T(1,128)} %bitcast.14, f32[1,128]{1,0:T(1,128)} %bitcast.18, f32[1,128]{1,0:T(1,128)} %bitcast.19, f32[4,1,512]{2,1,0:T(1,128)} %bitcast.15, f32[1,64]{1,0:T(1,128)} %constant.12.clone.freq, s32[9,32]{1,0:T(8,128)} %table.1, ...), custom_call_target="tpu_custom_call" | custom-call | tf_op jit(solution)/shard_map/pallas_call | solution.py:495
  151.7 1.6 %copy.27 = bf16[128,512]{1,0:T(8,128)(2,1)} copy(bf16[128,512]{1,0:T(8,128)(2,1)} %shard_map.235) | data formatting | bytes 262144

commit v3 on v2

--- a/solution.py
+++ b/solution.py
@@ -41,13 +41,13 @@
 def layer_kernel(
     nx, nz,
     lens, hid, gin, qgain, kgain, gpost, freq, table, ids_t, rw_t,
-    exp_t, slot_t, exp_r, slot_r, perm1, perm2,
+    home_t, slot_t, home_r, slot_r, perm1, perm2,
     qw, kw, vw, ow, kp, vp, wg_in, wu_in, wd_in,
     out,
     owner, cos_t, sin_t, xbuf, nbuf, qw_v, kw_v, vw_v, ow_v, kc, vc, q2, kn, vn, abuf,
-    rs_send, rs_recv, st_send, st_recv, nb, resid, s_mat, w_hi, w_lo,
-    send1, recv1, zbuf, xe, wg, wu, wd, ye, send2, recv2,
-    loc_s, ag_s, ag_r, rs_s, rs_r, st_s, st_r, d1_s, d1_r, d2_s, d2_r, w_s, w_r, f_s,
+    rs_send, rs_recv, st_send, st_recv, rbuf, resid, s_mat, w_hi, w_lo,
+    send1, recv1, ids_all, rw_all, xe, wg, wu, wd, hbuf, ye, send2, recv2, ring_out, ring_in,
+    loc_s, ag_s, ag_r, rs_s, rs_r, st_s, st_r, rb_s, rb_r, d1_s, d1_r, d2_s, d2_r, w_s, w_r, f_s, id_s, id_r, rg_s, rg_r,
 ):
     me_r = lax.axis_index("req")
     my = lax.axis_index("tp")
@@ -55,28 +55,26 @@
     chip = me_r // 2
     cx = chip // nz
     cz = lax.rem(chip, nz)
-    world = chip * 4 + my
-    n_world = nx * nz * 4
-    n_rows = n_world * CAP
+    n_chip = nx * nz
     src_slot = cz * nx + cx
+    ff = wd.shape[1]
 
     def peer(k):
         return lax.rem(my + k, 4)
 
     barrier = pltpu.get_barrier_semaphore()
 
-    def greet(k, carry):
-        other = lax.rem(world + k, n_world)
-        pl.semaphore_signal(
-            barrier, inc=1,
-            device_id={"req": (other // 4) * 2 + core, "tp": lax.rem(other, 4)},
-            device_id_type=MESH,
-        )
-        return carry
-
-    lax.fori_loop(1, n_world, greet, 0)
+    def greet(device):
+        pl.semaphore_signal(barrier, inc=1, device_id=device, device_id_type=MESH)
+
+    for k in range(1, n_chip):
+        greet({"req": lax.rem(chip + k, n_chip) * 2 + core})
+    for dx in range(nx):
+        for k in (1, 2, 3):
+            greet({"req": (lax.rem(cx + dx, nx) * nz + cz) * 2 + core, "tp": peer(k)})
     sibling = {"req": chip * 2 + 1 - core, "tp": my}
-    pl.semaphore_signal(barrier, inc=1, device_id=sibling, device_id_type=MESH)
+    greet(sibling)
+    n_peers = n_chip + 3 * nx
 
     loads = [
         pltpu.make_async_copy(s, d, loc_s.at[i])
@@ -90,21 +88,22 @@
 
     lane = iota((TOK, TOK), 1)
     sub = iota((TOK, TOK), 0)
-    named_t = jnp.zeros((TOK, TOK), F32)
-    dense_t = jnp.zeros((TOK, TOK), F32)
-    for k in range(8):
-        hit = (ids_t[k : k + 1, :] == sub).astype(F32)
-        named_t = named_t + hit
-        dense_t = dense_t + hit * rw_t[k : k + 1, :]
-    before = (sub < lane).astype(BF16)
-    rank_t = jnp.where(named_t > 0, mm(named_t.astype(BF16), before), -1.0)
-    s_mat[...] = (mm(exp_t[...], rank_t.astype(BF16)) == slot_t[...].astype(F32)).astype(BF16)
-    chosen = mm(rank_t.T.astype(BF16), exp_r[...]) == slot_r[...]
-    dense_w = dense_t.T
-    dw_hi = dense_w.astype(BF16)
-    dw_lo = (dense_w - dw_hi.astype(F32)).astype(BF16)
-    w_hi[...] = jnp.where(chosen, mm(dw_hi, exp_r[...]), 0.0).astype(BF16)
-    w_lo[...] = jnp.where(chosen, mm(dw_lo, exp_r[...]), 0.0).astype(BF16)
+
+    def routes(group_ids, group_rw):
+        named = jnp.zeros((TOK, TOK), F32)
+        dense = jnp.zeros((TOK, TOK), F32)
+        for k in range(8):
+            hit = (group_ids[k : k + 1, :] == sub).astype(F32)
+            named = named + hit
+            dense = dense + hit * group_rw[k : k + 1, :]
+        rank = mm(named.astype(BF16), (sub < lane).astype(BF16))
+        return jnp.where(named > 0, rank, -1.0), dense
+
+    homes = (home_t[...] + my == iota(home_t.shape, 1)).astype(BF16)
+    rank_t, _ = routes(ids_t[...], rw_t[...])
+    s_mat[...] = (mm(homes, rank_t.astype(BF16)) == slot_t[...]).astype(BF16)
+    ids_all[cz] = ids_t[...]
+    rw_all[cz] = rw_t[...]
 
     page = iota((POOL, MAXPG), 0)
     entry = iota((POOL, MAXPG), 1)
@@ -133,7 +132,7 @@
     cos_t[...] = jnp.concatenate([cosine, cosine], axis=1)
     sin_t[...] = jnp.concatenate([-sine, sine], axis=1)
 
-    pl.semaphore_wait(barrier, n_world)
+    pl.semaphore_wait(barrier, n_peers)
 
     def ag_copy(k):
         return pltpu.make_async_remote_copy(
@@ -144,25 +143,42 @@
     for k in (1, 3, 2):
         ag_copy(k).start()
 
+    def table_copies(k):
+        device = {"req": (cx * nz + lax.rem(cz + k, nz)) * 2 + core}
+        return [
+            pltpu.make_async_remote_copy(
+                src_ref=src, dst_ref=dst.at[cz], send_sem=id_s.at[i], recv_sem=id_r.at[i],
+                device_id=device, device_id_type=MESH,
+            )
+            for i, (src, dst) in enumerate([(ids_t, ids_all), (rw_t, rw_all)])
+        ]
+
+    for k in range(1, nz):
+        for copy in table_copies(k):
+            copy.start()
+
     w_pairs = ((wg_in, wg), (wu_in, wu), (wd_in, wd))
 
-    def w_remote(a, i):
-        return pltpu.make_async_remote_copy(
-            src_ref=w_pairs[a][0].at[i], dst_ref=w_pairs[a][1].at[my],
+    piece = ff // 3
+
+    def w_remote(a, i, rows):
+        return pltpu.make_async_remote_copy(
+            src_ref=w_pairs[a][0].at[i, rows], dst_ref=w_pairs[a][1].at[my, rows],
             send_sem=w_s.at[a, i], recv_sem=w_r.at[a, my],
             device_id={"tp": 2 * core + i}, device_id_type=MESH,
         )
 
-    def w_start(a):
+    def w_start(a, t):
+        rows = pl.ds(t * piece, piece)
         for i in range(2):
             @pl.when(2 * core + i != my)
             def _():
-                w_remote(a, i).start()
+                w_remote(a, i, rows).start()
 
             @pl.when(2 * core + i == my)
             def _():
                 pltpu.make_async_copy(
-                    w_pairs[a][0].at[i], w_pairs[a][1].at[my], w_r.at[a, my]
+                    w_pairs[a][0].at[i, rows], w_pairs[a][1].at[my, rows], w_r.at[a, my]
                 ).start()
 
     def w_forward(a, j):
@@ -181,11 +197,12 @@
     def w_pass_on(a):
         @pl.when(primary)
         def _():
-            for j in range(4):
-                w_wait(a, j)
-                w_forward(a, j).start()
-
-    w_start(0)
+            for off in (0, 1, 3, 2):
+                w_wait(a, peer(off))
+                w_forward(a, peer(off)).start()
+
+    w_start(0, 0)
+    w_start(0, 1)
 
     for k in (1, 3, 2):
         ag_copy(k).wait_recv()
@@ -257,11 +274,19 @@
         rs_copy(k).wait_recv()
         total = total + rs_recv[k - 1].astype(F32)
     resid[...] = total
+    rbuf[my] = total.astype(BF16)
     col = jnp.sum(total * total, axis=-1, keepdims=True)
     diag = sub == lane
     row = jnp.sum(jnp.where(diag, col, 0.0), axis=0, keepdims=True)
     st_send[...] = jnp.broadcast_to(row, (8, TOK))
 
+    def rb_copy(k):
+        return pltpu.make_async_remote_copy(
+            src_ref=rbuf.at[my], dst_ref=rbuf.at[my],
+            send_sem=rb_s.at[k - 1], recv_sem=rb_r.at[k - 1],
+            device_id={"tp": peer(k)}, device_id_type=MESH,
+        )
+
     def st_copy(k):
         return pltpu.make_async_remote_copy(
             src_ref=st_send, dst_ref=st_recv.at[k - 1],
@@ -271,121 +296,145 @@
 
     for k in (1, 3, 2):
         st_copy(k).start()
-    w_start(1)
-    w_start(2)
+        rb_copy(k).start()
+    w_start(0, 2)
+    for a in (1, 2):
+        for t in range(3):
+            w_start(a, t)
     for k in (1, 3, 2):
         st_copy(k).wait_recv()
+        rb_copy(k).wait_recv()
     row = st_send[0:1, :] + st_recv[0, 0:1, :] + st_recv[1, 0:1, :] + st_recv[2, 0:1, :]
     col = jnp.sum(jnp.where(diag, row, 0.0), axis=-1, keepdims=True)
-    nb[...] = (
-        resid[...] * lax.rsqrt(col * (1.0 / 2048.0) + NORM_EPS) * gpost[my]
-    ).astype(BF16)
+    row_scale = lax.rsqrt(col * (1.0 / 2048.0) + NORM_EPS)
+    for j in range(4):
+        nbuf[:, j * 512 : (j + 1) * 512] = (
+            rbuf[j].astype(F32) * row_scale * gpost[j]
+        ).astype(BF16)
 
     def dz_of(jj):
-        return lax.rem(nz // 2 + ((jj + 1) // 2) * (1 - 2 * lax.rem(jj, 2)) + nz, nz)
+        return lax.rem(nz // 2 + ((jj + 1) // 2) * (2 * lax.rem(jj, 2) - 1) + nz, nz)
+
+    def plane(jj):
+        return lax.rem(cz + dz_of(jj), nz)
 
     def chip_at(jj, dx):
-        return lax.rem(cx + dx, nx), lax.rem(cz + dz_of(jj), nz)
-
-    def d1_copy(jj, dx, k, local=False):
+        return lax.rem(cx + dx, nx), plane(jj)
+
+    def d1_copy(jj, dx, local=False):
         gx, gz = chip_at(jj, dx)
-        g = gx * nz + gz
-        src = send1.at[pl.ds(pl.multiple_of((g * 4 + peer(k)) * BLK, 16), BLK)]
-        dst = recv1.at[my, pl.ds(pl.multiple_of(src_slot * BLK, 16), BLK)]
+        src = send1.at[pl.ds(pl.multiple_of((gz * nx + gx) * BLK, 16), BLK)]
+        dst = recv1.at[pl.ds(pl.multiple_of(src_slot * BLK, 16), BLK)]
         if local:
             return pltpu.make_async_copy(src, dst, d1_r.at[jj])
         return pltpu.make_async_remote_copy(
             src_ref=src, dst_ref=dst, send_sem=d1_s, recv_sem=d1_r.at[jj],
-            device_id={"req": g * 2 + core, "tp": peer(k)}, device_id_type=MESH,
+            device_id={"req": (gx * nz + gz) * 2 + core}, device_id_type=MESH,
         )
 
     def d2_copy(jj, dx, k, local=False):
         gx, gz = chip_at(jj, dx)
         src = send2.at[peer(k), pl.ds(pl.multiple_of((gz * nx + gx) * BLK, 16), BLK)]
-        dst = recv2.at[pl.ds(pl.multiple_of(world * BLK, 16), BLK)]
+        dst = recv2.at[jj, pl.ds(pl.multiple_of((cx * 4 + my) * BLK, 16), BLK)]
         if local:
             return pltpu.make_async_copy(src, dst, d2_r.at[jj])
         return pltpu.make_async_remote_copy(
             src_ref=src, dst_ref=dst, send_sem=d2_s, recv_sem=d2_r.at[jj],
-            device_id={"req": (gx * nz + gz) * 2 + core, "tp": peer(k)}, device_id_type=MESH,
-        )
-
-    def send_all(copy_of, jj, last=False):
+            device_id={"req": (gx * nz + cz) * 2 + core, "tp": peer(k)}, device_id_type=MESH,
+        )
+
+    def send_back(jj):
+        for dx in (2, 1, 3, 0):
+            for k in (2, 1, 3, 0):
+                d2_copy(jj, dx, k, local=dx == 0 and k == 0).start()
+
+    def send_line(jj, last=False):
         for dx in range(nx):
-            for k in range(4):
-                copy_of(jj, dx, k, local=last and dx == 0 and k == 0).start()
+            d1_copy(jj, dx, local=last and dx == 0).start()
 
     def build(jj):
-        parts = []
-        for dx in range(nx):
-            gx, gz = chip_at(jj, dx)
-            at = pl.multiple_of((gx * nz + gz) * BLK, 16)
-            z = mm(s_mat[pl.ds(at, BLK), :], nb[...]).astype(BF16)
-            parts.append(jnp.concatenate([z[:, i * 128 : (i + 1) * 128] for i in range(4)], axis=0))
-        o = mm(perm2[...], jnp.concatenate(parts, axis=1)).astype(BF16)
-        for dx in range(nx):
-            gx, gz = chip_at(jj, dx)
-            at = pl.multiple_of((gx * nz + gz) * 4 * BLK, 16)
-            send1[pl.ds(at, 4 * BLK), :] = o[:, dx * 128 : (dx + 1) * 128]
+        gz = plane(jj)
+        z = mm(s_mat[pl.ds(pl.multiple_of(gz * BLK, 16), BLK), :], nbuf[...]).astype(BF16)
+        parts = jnp.concatenate([z[:, i * 512 : (i + 1) * 512] for i in range(4)], axis=0)
+        at = pl.multiple_of(gz * nx * BLK, 16)
+        send1[pl.ds(at, nx * BLK), :] = mm(perm2[...], parts).astype(BF16)
 
     build(0)
 
     def build_step(jj, carry):
         build(jj)
-        send_all(d1_copy, jj - 1)
+        send_line(jj - 1)
         return carry
 
     lax.fori_loop(1, nz, build_step, 0)
-    send_all(d1_copy, nz - 1, last=True)
+    send_line(nz - 1, last=True)
+
+    def d_wait(ref, sem):
+        pltpu.make_async_copy(ref, ref, sem).wait()
+
+    d_wait(ids_all.at[pl.ds(0, nz - 1)], id_r.at[0])
+    d_wait(rw_all.at[pl.ds(0, nz - 1)], id_r.at[1])
+    spread = (home_r[...] + 4 * cz == iota((TOK, home_r.shape[1]), 0)).astype(BF16)
+
+    def weigh(jj, carry):
+        gz = plane(jj)
+        rank_t, dense_t = routes(ids_all[gz], rw_all[gz])
+        chosen = mm(rank_t.T.astype(BF16), spread) == slot_r[...]
+        dense_w = dense_t.T
+        dw_hi = dense_w.astype(BF16)
+        dw_lo = (dense_w - dw_hi.astype(F32)).astype(BF16)
+        w_hi[jj] = jnp.where(chosen, mm(dw_hi, spread), 0.0).astype(BF16)
+        w_lo[jj] = jnp.where(chosen, mm(dw_lo, spread), 0.0).astype(BF16)
+        return carry
+
+    lax.fori_loop(0, nz, weigh, 0)
 
     w_pass_on(0)
     w_pass_on(1)
-    w_pass_on(2)
-
-    def d_wait(ref, sem):
-        pltpu.make_async_copy(ref, ref, sem).wait()
-
-    for jj in range(nz):
-        d_wait(recv1.at[0, pl.ds(0, 4 * nx * BLK)], d1_r.at[jj])
-
-    def unpack(gz, carry):
-        at = pl.multiple_of(gz * nx * BLK, 16)
-        x = jnp.concatenate([recv1[q, pl.ds(at, nx * BLK), :] for q in range(4)], axis=1)
-        o = mm(perm1[...], x).astype(BF16)
-        to = pl.multiple_of(gz * BLK, 16)
-        for q in range(4):
-            for i in range(4):
-                xe[pl.ds(to, BLK), (q * 4 + i) * 128 : (q * 4 + i + 1) * 128] = o[
-                    i * BLK : (i + 1) * BLK, q * 128 : (q + 1) * 128
-                ]
-        return carry
-
-    lax.fori_loop(0, nz, unpack, 0)
-
-    @pl.when(jnp.logical_not(primary))
-    def _():
-        for a in range(3):
+
+    def w_wait_all(a):
+        @pl.when(jnp.logical_not(primary))
+        def _():
             for j in range(4):
                 w_wait(a, j)
 
-    half_rows = nx * nz * CAP // 2
-    ye[...] = jnp.zeros_like(ye)
-
-    def expert_step(t, carry):
-        j = t // 2
-        rows = pl.ds(pl.multiple_of(lax.rem(t, 2) * half_rows, 16), half_rows)
-        x = xe[rows, :]
-        gate = mm_t(x, wg[j])
-        up = mm_t(x, wu[j])
-        act = (gate / (1.0 + jnp.exp(-gate)) * up).astype(BF16)
-        ye[rows, :] += mm(act, wd[j])
+    def unpack(jj, carry):
+        gz = plane(jj)
+        o = mm(perm1[...], recv1[pl.ds(pl.multiple_of(gz * nx * BLK, 16), nx * BLK), :]).astype(BF16)
+        to = pl.multiple_of(jj * BLK, 16)
+        for i in range(4):
+            xe[pl.ds(to, BLK), i * 512 : (i + 1) * 512] = o[i * BLK : (i + 1) * BLK, :]
         return carry
 
-    lax.fori_loop(0, 8, expert_step, 0)
+    steps = [(nz // 2 + (j + 1) // 2 * (2 * (j % 2) - 1)) % nz for j in range(nz)]
+    from_sem = [steps.index((nz - d) % nz) for d in steps]
+    half_rows = n_chip * CAP // 2
+
+    for half in range(2):
+        first = half * (nz // 2)
+        for jj in range(first, first + nz // 2):
+            d_wait(recv1.at[pl.ds(0, nx * BLK)], d1_r.at[from_sem[jj]])
+        lax.fori_loop(first, first + nz // 2, unpack, 0)
+        if half == 0:
+            w_wait_all(0)
+            w_wait_all(1)
+        rows = pl.ds(half * half_rows, half_rows)
+
+        def act_step(j, carry):
+            x = xe[rows, :]
+            gate = mm_t(x, wg[j])
+            up = mm_t(x, wu[j])
+            hbuf[j, rows, :] = (gate / (1.0 + jnp.exp(-gate)) * up).astype(BF16)
+            return carry
+
+        lax.fori_loop(0, 4, act_step, 0)
+        if half == 0:
+            w_pass_on(2)
+    w_wait_all(2)
 
     def pack(jj):
-        gz = lax.rem(cz + dz_of(jj), nz)
-        rows = pl.ds(pl.multiple_of(gz * BLK, 16), BLK)
+        gz = plane(jj)
+        rows = pl.ds(pl.multiple_of(jj * BLK, 16), BLK)
         parts = []
         for i in range(4):
             parts.append(
@@ -398,46 +447,72 @@
         for q in range(4):
             send2[q, pl.ds(at, nx * BLK), :] = o[:, q * 128 : (q + 1) * 128]
 
-    pack(0)
-
-    def pack_step(jj, carry):
-        pack(jj)
-        send_all(d2_copy, jj - 1)
-        return carry
-
-    lax.fori_loop(1, nz, pack_step, 0)
-    send_all(d2_copy, nz - 1, last=True)
-
-    for jj in range(nz):
-        d_wait(recv2.at[pl.ds(0, 4 * nx * BLK)], d2_r.at[jj])
-
-    def collect(b, carry):
+    for half in range(2):
+        rows = pl.ds(half * half_rows, half_rows)
+        ye[rows, :] = mm(hbuf[0, rows, :], wd[0])
+
+        def down_step(j, carry):
+            ye[rows, :] += mm(hbuf[j, rows, :], wd[j])
+            return carry
+
+        lax.fori_loop(1, 4, down_step, 0)
+        first = half * (nz // 2)
+        pack(first)
+
+        def pack_step(jj, carry):
+            pack(jj)
+            send_back(jj - 1)
+            return carry
+
+        lax.fori_loop(first + 1, first + nz // 2, pack_step, 0)
+        send_back(first + nz // 2 - 1)
+
+    def ring_copy(jj):
+        step = 1 if jj % 2 == 0 else nz - 1
+        return pltpu.make_async_remote_copy(
+            src_ref=ring_out.at[jj], dst_ref=ring_in.at[jj],
+            send_sem=rg_s.at[jj], recv_sem=rg_r.at[jj],
+            device_id={"req": (cx * nz + lax.rem(cz + step, nz)) * 2 + core}, device_id_type=MESH,
+        )
+
+    def partial_sum(jj):
+        d_wait(recv2.at[jj], d2_r.at[jj])
         x = jnp.concatenate(
-            [recv2[pl.ds(pl.multiple_of((b * 4 + i) * 4 * BLK, 16), 4 * BLK), :] for i in range(4)],
-            axis=1,
+            [recv2[jj, i * 4 * BLK : (i + 1) * 4 * BLK, :] for i in range(nx)], axis=1
         )
         o = mm(perm1[...], x).astype(BF16)
-        for i in range(4):
-            to = pl.multiple_of((b * 4 + i) * BLK, 16)
-            for q in range(4):
-                zbuf[pl.ds(to, BLK), q * 128 : (q + 1) * 128] = o[
-                    q * BLK : (q + 1) * BLK, i * 128 : (i + 1) * 128
-                ]
-        return carry
-
-    lax.fori_loop(0, nx * nz // 4, collect, 0)
-    moe = mm(w_hi[...], zbuf[...]) + mm(w_lo[...], zbuf[...])
+        rows = [
+            jnp.concatenate(
+                [o[q * BLK : (q + 1) * BLK, i * 128 : (i + 1) * 128] for q in range(4)], axis=1
+            )
+            for i in range(nx)
+        ]
+        back = jnp.concatenate(rows, axis=0)
+        return mm(w_hi[jj], back) + mm(w_lo[jj], back)
+
+    for jj in range(nz - 1):
+        part = partial_sum(jj)
+        if jj >= 2:
+            ring_copy(jj - 2).wait_recv()
+            part = part + ring_in[jj - 2].astype(F32)
+        ring_out[jj] = part.astype(BF16)
+        ring_copy(jj).start()
+    moe = partial_sum(nz - 1)
+    for jj in (nz - 3, nz - 2):
+        ring_copy(jj).wait_recv()
+        moe = moe + ring_in[jj].astype(F32)
     out[...] = (resid[...] + moe).astype(BF16)
 
     for k in (1, 2, 3):
         ag_copy(k).wait_send()
         rs_copy(k).wait_send()
         st_copy(k).wait_send()
+        rb_copy(k).wait_send()
     for a in range(3):
         for i in range(2):
             @pl.when(2 * core + i != my)
             def _():
-                w_remote(a, i).wait_send()
+                w_remote(a, i, pl.ds(0, ff)).wait_send()
 
     @pl.when(primary)
     def _():
@@ -445,9 +520,13 @@
             for j in range(4):
                 w_forward(a, j).wait_send()
 
-    sent = pl.ds(0, (n_world - 1) * BLK)
-    d_wait(send1.at[sent], d1_s)
-    d_wait(recv2.at[sent], d2_s)
+    d_wait(send1.at[pl.ds(0, (nx * nz - 1) * BLK)], d1_s)
+    for jj in range(nz):
+        d_wait(recv2.at[0, pl.ds(0, (nx * 4 - 1) * BLK)], d2_s)
+    for jj in range(nz - 1):
+        ring_copy(jj).wait_send()
+    d_wait(ids_all.at[pl.ds(0, nz - 1)], id_s.at[0])
+    d_wait(rw_all.at[pl.ds(0, nz - 1)], id_s.at[1])
 
 
 def perm_tables():
@@ -465,23 +544,24 @@
     gate_weight, up_weight, down_weight,
 ):
     n_chip = nx * nz
-    n_world = n_chip * 4
-    n_rows = n_world * CAP
     width = hidden_in.shape[1]
     model = norm_in_gain.shape[0]
     ff = gate_weight.shape[2]
     half = np.arange(64, dtype=np.float64)
     freq = np.power(ROPE_BASE, -2.0 * half / 128.0)
-    slots = np.arange(n_rows)
-    exp_t = (slots[:, None] // CAP == np.arange(TOK)[None, :]).astype(np.float32)
-    slot_t = np.broadcast_to((slots % CAP)[:, None], (n_rows, TOK)).astype(np.float32)
+    slots = np.arange(nx * 4 * CAP)
+    home_r = slots // (4 * CAP) * nz * 4 + slots // CAP % 4
+    line = np.arange(n_chip * CAP) // CAP
+    home = ((line % nx) * nz + line // nx) * 4
+    home_t = np.broadcast_to(home[:, None], (n_chip * CAP, TOK))
+    slot_t = np.broadcast_to((np.arange(n_chip * CAP) % CAP)[:, None], (n_chip * CAP, TOK))
     p1, p2 = perm_tables()
     small = [
         hidden_in, norm_in_gain[None, :], q_gain[None, :], k_gain[None, :],
         norm_post_gain.reshape(4, 1, width), jnp.asarray(freq[None, :], F32), page_table,
         expert_ids.T, route_weights.T,
-        jnp.asarray(exp_t, BF16), jnp.asarray(slot_t, BF16), jnp.asarray(exp_t.T, BF16),
-        jnp.asarray((slots % CAP)[None, :], F32), jnp.asarray(p1, BF16), jnp.asarray(p2, BF16),
+        jnp.asarray(home_t, jnp.int32), jnp.asarray(slot_t, F32),
+        jnp.asarray(home_r[None, :], jnp.int32), jnp.asarray((slots % CAP)[None, :], F32), jnp.asarray(p1, BF16), jnp.asarray(p2, BF16),
     ]
     cache = POOL * PAGE
     large = [
@@ -507,15 +587,17 @@
             vmem((4 * TOK, 128)), vmem((TOK, 128)), vmem((TOK, 128)), vmem((TOK, 512)),
             vmem((4, TOK, width)), vmem((3, TOK, width)),
             vmem((8, TOK), F32), vmem((3, 8, TOK), F32),
-            vmem((TOK, width)), vmem((TOK, width), F32),
-            vmem((n_rows, TOK)), vmem((TOK, n_rows)), vmem((TOK, n_rows)),
-            vmem((n_world * BLK, 128)), vmem((4, n_chip * BLK, 128)),
-            vmem((n_rows, width)), vmem((rows, model)),
+            vmem((4, TOK, width)), vmem((TOK, width), F32),
+            vmem((rows, TOK)), vmem((nz, TOK, nx * 4 * CAP)), vmem((nz, TOK, nx * 4 * CAP)),
+            vmem((n_chip * BLK, width)), vmem((n_chip * BLK, width)),
+            vmem((nz, 8, TOK), jnp.int32), vmem((nz, 8, TOK), F32), vmem((rows, model)),
             vmem((4, ff, model)), vmem((4, ff, model)), vmem((4, ff, model)),
-            vmem((rows, model), F32),
-            vmem((4, n_chip * BLK, 128)), vmem((n_world * BLK, 128)),
+            vmem((4, rows, ff)), vmem((rows, model), F32),
+            vmem((4, n_chip * BLK, 128)), vmem((nz, nx * 4 * BLK, 128)),
+            vmem((nz - 1, TOK, width)), vmem((nz - 1, TOK, width)),
             dma((6,)), dma((3,)), dma((3,)), dma((3,)), dma((3,)), dma((3,)), dma((3,)),
-            dma, dma((nz,)), dma, dma((nz,)), dma((3, 2)), dma((3, 4)), dma((3, 4)),
+            dma((3,)), dma((3,)), dma, dma((nz,)), dma, dma((nz,)), dma((3, 2)), dma((3, 4)), dma((3, 4)),
+            dma((2,)), dma((2,)), dma((nz - 1,)), dma((nz - 1,)),
         ],
         compiler_params=pltpu.CompilerParams(
             collective_id=0, has_side_effects=True, vmem_limit_bytes=62 * 1024 * 1024

time: 153 us -> 117 us (0.76)
  Pallas kernels: 152 us -> 115 us
    pallas_call x1, Pallas kernels: 152 us -> 115 us  [body(): pl.pallas_call(functools.partial(layer_kernel, nx, nz), out_shape=jax.Sha...]
where the time goes in v3:
time: 117 us
  Pallas kernels  115 us (98%)
  local copies, waits for them, and re-layouts  1.57 us (1%)
    pallas_call x1, Pallas kernels, body(): pl.pallas_call(functools.partial(layer_kernel, nx, nz), out_shape=jax.Sha...  115 us

profile of v3, /device:TPU:1, one launch (start us, length us, event | category | flops | bytes accessed | tf_op | source)
XLA Modules:
  0.0 117.0 jit_solution(12924334837393852361)
XLA Ops:
  0.0 115.4 %shard_map.235 = bf16[128,512]{1,0:T(8,128)(2,1)} custom-call(s32[9]{0:T(128)} %lens.1, bf16[128,512]{1,0:T(8,128)(2,1)} %hid.1, f32[1,2048]{1,0:T(1,128)} %bitcast.14, f32[1,128]{1,0:T(1,128)} %bitcast.18, f32[1,128]{1,0:T(1,128)} %bitcast.19, f32[4,1,512]{2,1,0:T(1,128)} %bitcast.15, f32[1,64]{1,0:T(1,128)} %constant.12.clone.freq, s32[9,32]{1,0:T(8,128)} %table.1, ...), custom_call_target="tpu_custom_call" | custom-call | tf_op jit(solution)/shard_map/pallas_call | solution.py:575
  115.4 1.6 %copy.27 = bf16[128,512]{1,0:T(8,128)(2,1)} copy(bf16[128,512]{1,0:T(8,128)(2,1)} %shard_map.235) | data formatting | bytes 262144

commit v4 on v3

--- a/solution.py
+++ b/solution.py
@@ -194,10 +194,10 @@
 
     primary = core == my // 2
 
-    def w_pass_on(a):
+    def w_pass_on(a, offs=(0, 1, 3, 2)):
         @pl.when(primary)
         def _():
-            for off in (0, 1, 3, 2):
+            for off in offs:
                 w_wait(a, peer(off))
                 w_forward(a, peer(off)).start()
 
@@ -217,21 +217,23 @@
         v = v * lax.rsqrt(ms + NORM_EPS) * gain
         return (v * cos_t[...] + pltpu.roll(v, 64, 1) * sin_t[...]).astype(BF16)
 
+    score_scale = math.log2(math.e) / math.sqrt(128)
     q_lin = mm(nbuf[...], qw_v[...])
     for g in range(4):
-        q2[g * TOK : (g + 1) * TOK, :] = head_norm(q_lin[:, g * 128 : (g + 1) * 128], qgain[...])
+        q2[g * TOK : (g + 1) * TOK, :] = head_norm(
+            q_lin[:, g * 128 : (g + 1) * 128], qgain[...] * score_scale
+        )
     kn[...] = head_norm(mm(nbuf[...], kw_v[...]), kgain[...])
     vn[...] = mm(nbuf[...], vw_v[...]).astype(BF16)
 
-    inv_root = 1.0 / math.sqrt(128)
     n_q = 4 * TOK
     row_tok = lax.rem(iota((n_q, 1), 0), TOK)
     row_req = jnp.where(row_tok < PRE, 0, row_tok - PRE + 1)
     key_tok = iota((n_q, TOK), 1)
     new_mask = (key_tok == row_tok) | ((row_tok < PRE) & (key_tok <= row_tok))
-    sc = jnp.where(new_mask, mm_t(q2[...], kn[...]) * inv_root, -1e30)
+    sc = jnp.where(new_mask, mm_t(q2[...], kn[...]), -1e30)
     m0 = jnp.max(sc, axis=-1, keepdims=True)
-    pr = jnp.exp(sc - m0)
+    pr = jnp.exp2(sc - m0)
     l0 = jnp.sum(pr, axis=-1, keepdims=True)
     acc0 = mm(pr.astype(BF16), vn[...])
     for load in loads[3:5]:
@@ -240,19 +242,21 @@
     def attend_chunk(j, carry):
         m, l, acc = carry
         at = pl.multiple_of(j * CHUNK, CHUNK)
-        s = mm_t(q2[...], kc[pl.ds(at, CHUNK), :]) * inv_root
+        s = mm_t(q2[...], kc[pl.ds(at, CHUNK), :])
         own = jnp.concatenate(
             [owner[pl.ds(j * (CHUNK // PAGE) + i, 1), :] for i in range(CHUNK // PAGE)], axis=1
         )
         s = jnp.where(own == row_req, s, -1e30)
         m_new = jnp.maximum(m, jnp.max(s, axis=-1, keepdims=True))
-        scale = jnp.exp(m - m_new)
-        p = jnp.exp(s - m_new)
+        scale = jnp.exp2(m - m_new)
+        p = jnp.exp2(s - m_new)
         l = l * scale + jnp.sum(p, axis=-1, keepdims=True)
         acc = acc * scale + mm(p.astype(BF16), vc[pl.ds(at, CHUNK), :])
         return m_new, l, acc
 
-    _, l_all, acc_all = lax.fori_loop(0, POOL * PAGE // CHUNK, attend_chunk, (m0, l0, acc0))
+    _, l_all, acc_all = lax.fori_loop(
+        0, POOL * PAGE // CHUNK, attend_chunk, (m0, l0, acc0), unroll=4
+    )
     att = (acc_all / l_all).astype(BF16)
     for g in range(4):
         abuf[:, g * 128 : (g + 1) * 128] = att[g * TOK : (g + 1) * TOK, :]
@@ -391,6 +395,7 @@
 
     w_pass_on(0)
     w_pass_on(1)
+    w_pass_on(2, (0,))
 
     def w_wait_all(a):
         @pl.when(jnp.logical_not(primary))
@@ -414,6 +419,8 @@
         first = half * (nz // 2)
         for jj in range(first, first + nz // 2):
             d_wait(recv1.at[pl.ds(0, nx * BLK)], d1_r.at[from_sem[jj]])
+        if half == 1:
+            w_pass_on(2, (1, 3, 2))
         lax.fori_loop(first, first + nz // 2, unpack, 0)
         if half == 0:
             w_wait_all(0)
@@ -428,8 +435,6 @@
             return carry
 
         lax.fori_loop(0, 4, act_step, 0)
-        if half == 0:
-            w_pass_on(2)
     w_wait_all(2)
 
     def pack(jj):

time: 117 us -> 115 us (0.983)
  Pallas kernels: 115 us -> 113 us
    pallas_call x1, Pallas kernels: 115 us -> 113 us  [body(): pl.pallas_call(functools.partial(layer_kernel, nx, nz), out_shape=jax.Sha...]
where the time goes in v4:
time: 115 us; the launch traced here: 114 us
  Pallas kernels  113 us (98%)
  local copies, waits for them, and re-layouts  1.57 us (1%)
    pallas_call x1, Pallas kernels, body(): pl.pallas_call(functools.partial(layer_kernel, nx, nz), out_shape=jax.Sha...  113 us

profile of v4, /device:TPU:1, one launch (start us, length us, event | category | flops | bytes accessed | tf_op | source)
XLA Modules:
  0.0 114.1 jit_solution(16526742228844803423)
XLA Ops:
  0.0 112.6 %shard_map.235 = bf16[128,512]{1,0:T(8,128)(2,1)} custom-call(s32[9]{0:T(128)} %lens.1, bf16[128,512]{1,0:T(8,128)(2,1)} %hid.1, f32[1,2048]{1,0:T(1,128)} %bitcast.14, f32[1,128]{1,0:T(1,128)} %bitcast.18, f32[1,128]{1,0:T(1,128)} %bitcast.19, f32[4,1,512]{2,1,0:T(1,128)} %bitcast.15, f32[1,64]{1,0:T(1,128)} %constant.12.clone.freq, s32[9,32]{1,0:T(8,128)} %table.1, ...), custom_call_target="tpu_custom_call" | custom-call | tf_op jit(solution)/shard_map/pallas_call | solution.py:580
  112.6 1.6 %copy.27 = bf16[128,512]{1,0:T(8,128)(2,1)} copy(bf16[128,512]{1,0:T(8,128)(2,1)} %shard_map.235) | data formatting | bytes 262144

commit v5 on v4

--- a/solution.py
+++ b/solution.py
@@ -24,6 +24,8 @@
 BF16 = jnp.bfloat16
 BLK = 48
 CHUNK = 512
+PIECES = 6
+EARLY = 3
 
 
 def mm(a, b):
@@ -159,12 +161,15 @@
 
     w_pairs = ((wg_in, wg), (wu_in, wu), (wd_in, wd))
 
-    piece = ff // 3
-
-    def w_remote(a, i, rows):
+    piece = ff // PIECES
+
+    def slot(a, t):
+        return t if a == 2 else 0
+
+    def w_remote(a, i, t, rows):
         return pltpu.make_async_remote_copy(
             src_ref=w_pairs[a][0].at[i, rows], dst_ref=w_pairs[a][1].at[my, rows],
-            send_sem=w_s.at[a, i], recv_sem=w_r.at[a, my],
+            send_sem=w_s.at[a, i], recv_sem=w_r.at[a, my, slot(a, t)],
             device_id={"tp": 2 * core + i}, device_id_type=MESH,
         )
 
@@ -173,36 +178,42 @@
         for i in range(2):
             @pl.when(2 * core + i != my)
             def _():
-                w_remote(a, i, rows).start()
+                w_remote(a, i, t, rows).start()
 
             @pl.when(2 * core + i == my)
             def _():
                 pltpu.make_async_copy(
-                    w_pairs[a][0].at[i, rows], w_pairs[a][1].at[my, rows], w_r.at[a, my]
+                    w_pairs[a][0].at[i, rows],
+                    w_pairs[a][1].at[my, rows],
+                    w_r.at[a, my, slot(a, t)],
                 ).start()
 
-    def w_forward(a, j):
-        return pltpu.make_async_remote_copy(
-            src_ref=w_pairs[a][1].at[j], dst_ref=w_pairs[a][1].at[j],
-            send_sem=f_s.at[a, j], recv_sem=w_r.at[a, j],
+    def w_part(a, j, t):
+        rows = pl.ds(t * piece, piece) if a == 2 else pl.ds(0, ff)
+        return w_pairs[a][1].at[j, rows]
+
+    def w_forward(a, j, t):
+        ref = w_part(a, j, t)
+        return pltpu.make_async_remote_copy(
+            src_ref=ref, dst_ref=ref, send_sem=f_s.at[a, j], recv_sem=w_r.at[a, j, t],
             device_id=sibling, device_id_type=MESH,
         )
 
-    def w_wait(a, j):
-        ref = w_pairs[a][1].at[j]
-        pltpu.make_async_copy(ref, ref, w_r.at[a, j]).wait()
+    def w_wait(a, j, t):
+        ref = w_part(a, j, t)
+        pltpu.make_async_copy(ref, ref, w_r.at[a, j, t]).wait()
 
     primary = core == my // 2
 
-    def w_pass_on(a, offs=(0, 1, 3, 2)):
+    def w_pass_on(a, t, offs=(0, 1, 3, 2)):
         @pl.when(primary)
         def _():
             for off in offs:
-                w_wait(a, peer(off))
-                w_forward(a, peer(off)).start()
-
-    w_start(0, 0)
-    w_start(0, 1)
+                w_wait(a, peer(off), t)
+                w_forward(a, peer(off), t).start()
+
+    for t in range(EARLY):
+        w_start(0, t)
 
     for k in (1, 3, 2):
         ag_copy(k).wait_recv()
@@ -301,9 +312,10 @@
     for k in (1, 3, 2):
         st_copy(k).start()
         rb_copy(k).start()
-    w_start(0, 2)
+    for t in range(EARLY, PIECES):
+        w_start(0, t)
     for a in (1, 2):
-        for t in range(3):
+        for t in range(PIECES):
             w_start(a, t)
     for k in (1, 3, 2):
         st_copy(k).wait_recv()
@@ -393,15 +405,17 @@
 
     lax.fori_loop(0, nz, weigh, 0)
 
-    w_pass_on(0)
-    w_pass_on(1)
-    w_pass_on(2, (0,))
+    w_pass_on(0, 0)
+    w_pass_on(1, 0)
+    for t in range(PIECES):
+        w_pass_on(2, t, (0,))
 
     def w_wait_all(a):
         @pl.when(jnp.logical_not(primary))
         def _():
             for j in range(4):
-                w_wait(a, j)
+                for t in range(PIECES if a == 2 else 1):
+                    w_wait(a, j, t)
 
     def unpack(jj, carry):
         gz = plane(jj)
@@ -420,7 +434,8 @@
         for jj in range(first, first + nz // 2):
             d_wait(recv1.at[pl.ds(0, nx * BLK)], d1_r.at[from_sem[jj]])
         if half == 1:
-            w_pass_on(2, (1, 3, 2))
+            for t in range(PIECES // 3, PIECES - 2):
+                w_pass_on(2, t, (1, 3, 2))
         lax.fori_loop(first, first + nz // 2, unpack, 0)
         if half == 0:
             w_wait_all(0)
@@ -434,7 +449,15 @@
             hbuf[j, rows, :] = (gate / (1.0 + jnp.exp(-gate)) * up).astype(BF16)
             return carry
 
-        lax.fori_loop(0, 4, act_step, 0)
+        if half == 0:
+            lax.fori_loop(0, 4, act_step, 0)
+            for t in range(PIECES // 3):
+                w_pass_on(2, t, (1, 3, 2))
+        else:
+            for step in range(2):
+                act_step(step, 0)
+                w_pass_on(2, PIECES - 2 + step, (1, 3, 2))
+            lax.fori_loop(2, 4, act_step, 0)
     w_wait_all(2)
 
     def pack(jj):
@@ -517,13 +540,14 @@
         for i in range(2):
             @pl.when(2 * core + i != my)
             def _():
-                w_remote(a, i, pl.ds(0, ff)).wait_send()
+                w_remote(a, i, 0, pl.ds(0, ff)).wait_send()
 
     @pl.when(primary)
     def _():
         for a in range(3):
             for j in range(4):
-                w_forward(a, j).wait_send()
+                for t in range(PIECES if a == 2 else 1):
+                    w_forward(a, j, t).wait_send()
 
     d_wait(send1.at[pl.ds(0, (nx * nz - 1) * BLK)], d1_s)
     for jj in range(nz):
@@ -601,7 +625,7 @@
             vmem((4, n_chip * BLK, 128)), vmem((nz, nx * 4 * BLK, 128)),
             vmem((nz - 1, TOK, width)), vmem((nz - 1, TOK, width)),
             dma((6,)), dma((3,)), dma((3,)), dma((3,)), dma((3,)), dma((3,)), dma((3,)),
-            dma((3,)), dma((3,)), dma, dma((nz,)), dma, dma((nz,)), dma((3, 2)), dma((3, 4)), dma((3, 4)),
+            dma((3,)), dma((3,)), dma, dma((nz,)), dma, dma((nz,)), dma((3, 2)), dma((3, 4, PIECES)), dma((3, 4)),
             dma((2,)), dma((2,)), dma((nz - 1,)), dma((nz - 1,)),
         ],
         compiler_params=pltpu.CompilerParams(

time: 115 us -> 114 us (level)
  no operation moved by 1% of the time
where the time goes in v5:
time: 114 us; the launch traced here: 113 us
  Pallas kernels  112 us (98%)
  local copies, waits for them, and re-layouts  1.57 us (1%)
    pallas_call x1, Pallas kernels, body(): pl.pallas_call(functools.partial(layer_kernel, nx, nz), out_shape=jax.Sha...  112 us

profile of v5, /device:TPU:1, one launch (start us, length us, event | category | flops | bytes accessed | tf_op | source)
XLA Modules:
  0.0 113.3 jit_solution(2215596254763956243)
XLA Ops:
  0.0 111.8 %shard_map.235 = bf16[128,512]{1,0:T(8,128)(2,1)} custom-call(s32[9]{0:T(128)} %lens.1, bf16[128,512]{1,0:T(8,128)(2,1)} %hid.1, f32[1,2048]{1,0:T(1,128)} %bitcast.14, f32[1,128]{1,0:T(1,128)} %bitcast.18, f32[1,128]{1,0:T(1,128)} %bitcast.19, f32[4,1,512]{2,1,0:T(1,128)} %bitcast.15, f32[1,64]{1,0:T(1,128)} %constant.12.clone.freq, s32[9,32]{1,0:T(8,128)} %table.1, ...), custom_call_target="tpu_custom_call" | custom-call | tf_op jit(solution)/shard_map/pallas_call | solution.py:604
  111.8 1.6 %copy.27 = bf16[128,512]{1,0:T(8,128)(2,1)} copy(bf16[128,512]{1,0:T(8,128)(2,1)} %shard_map.235) | data formatting | bytes 262144
